TPU v7x, 256 devices: a whole 4x4x8 slice. The times are simulated.
256 devices in a mesh: peer: 8 (over x, z_hi), depth: 4 (over z_lo), row: 8 (over y, core).
Axes of the slice: x: 4, y: 4, z: 8 (z_hi: 2, z_lo: 4; z = z_hi * 4 + z_lo), core: 2. Of those that a mesh axis runs over, the one named last changes fastest.
Arguments:
- features: bfloat16 [12, 64, 2048], P('depth', 'row'), may hold values from -6 to 6
- labels: int32 [12, 64, 64], P('depth', 'row'), may hold values from 0 to 103
- conv_weights: bfloat16 [8, 4, 864, 32], P('peer'), may hold values from -0.21875 to 0.21875
- head_weights: bfloat16 [8, 32, 104], P('peer'), may hold values from -4 to 4
- matching: int32 [12, 8], P('depth'), may hold values from 0 to 7, each once within a row
Outputs:
- conv_grads: float32 [8, 4, 864, 32], P('peer')
- head_grads: float32 [8, 32, 104], P('peer')
- input_grads: bfloat16 [8, 12, 64, 2048], P('peer', 'depth', 'row')
Inputs may be any that keep to these rules, and one draw needn't show every extreme that they name: `matching`: in every depth plane every peer is distilled by exactly one peer.
All inputs are finite; a program needn't handle non-finite values.
Results may differ from a plain program's by a relative error of at most 0.019.
Values may be sent and summed in bfloat16 or wider, within the bound.
A program may use at most 64 MiB of HBM per device.

v0:
```python
import jax
import jax.numpy as jnp
from jax import lax
from jax.sharding import PartitionSpec as P


def with_halo(cells, sides, width):
    for axis, dim in sides:
        count = lax.axis_size(axis)
        ends = count - 1
        head = lax.slice_in_dim(cells, 0, width, axis=dim)
        tail = lax.slice_in_dim(cells, cells.shape[dim] - width, cells.shape[dim], axis=dim)
        cells = jnp.concatenate(
            [
                lax.ppermute(tail, axis, [(i, (i + 1) % count) for i in range(ends)]),
                cells,
                lax.ppermute(head, axis, [((i + 1) % count, i) for i in range(ends)]),
            ],
            axis=dim,
        )
    return cells


def columns(block, rows_out, width_out):
    pieces = []
    for depth_off in range(3):
        for row_off in range(3):
            for col_off in range(3):
                pieces.append(
                    block[depth_off, row_off : row_off + rows_out, col_off : col_off + width_out, :]
                )
    return jnp.concatenate(pieces, axis=-1).reshape(rows_out * width_out, -1)


def widened(padded, channels):
    depth_in, rows_in, merged = padded.shape
    volume = padded.reshape(depth_in, rows_in, merged // channels, channels)
    return jnp.pad(volume, ((0, 0), (0, 0), (1, 1), (0, 0)))


def convolve(padded, weight):
    channels = weight.shape[1]
    volume = widened(padded, channels)
    depth_out = padded.shape[0] - 2
    rows_out = padded.shape[1] - 2
    width_out = volume.shape[2] - 2

    def one_slice(depth_index):
        block = lax.dynamic_slice_in_dim(volume, depth_index, 3, 0)
        return jnp.dot(
            columns(block, rows_out, width_out), weight, preferred_element_type=jnp.float32
        )

    result = lax.map(one_slice, jnp.arange(depth_out, dtype=jnp.int32))
    return result.reshape(depth_out, rows_out, width_out * channels)


def weight_grad(padded, grad_out, channels):
    volume = widened(padded, channels)
    depth_out = padded.shape[0] - 2
    rows_out = padded.shape[1] - 2
    width_out = volume.shape[2] - 2
    grads = grad_out.reshape(depth_out, rows_out * width_out, channels)

    def accumulate(carry, depth_index):
        block = lax.dynamic_slice_in_dim(volume, depth_index, 3, 0)
        cols = columns(block, rows_out, width_out)
        slab = lax.dynamic_index_in_dim(grads, depth_index, 0, keepdims=False)
        contrib = lax.dot_general(
            cols, slab, (((0,), (0,)), ((), ())), preferred_element_type=jnp.float32
        )
        return (carry + contrib, None)

    init = jnp.zeros((27 * channels, channels), jnp.float32)
    result, unused = lax.scan(accumulate, init, jnp.arange(depth_out, dtype=jnp.int32))
    return result


def flipped(weight):
    channels = weight.shape[1]
    return (
        weight.reshape(27, channels, channels)[::-1]
        .transpose(0, 2, 1)
        .reshape(27 * channels, channels)
    )


def slope(pre):
    value = pre.astype(jnp.float32)
    sigma = jax.nn.sigmoid(value)
    return sigma * (1.0 + value * (1.0 - sigma))


def softmax_rows(hidden, head):
    logits = jnp.dot(hidden, head, preferred_element_type=jnp.float32)
    exponent = jnp.exp(logits)
    return exponent / jnp.sum(exponent, axis=1, keepdims=True)


def body(features, labels, conv_weights, head_weights, matching):
    channels = conv_weights.shape[3]
    classes = head_weights.shape[2]
    layers = conv_weights.shape[1]
    slab_depth, slab_rows, merged = features.shape
    width_cells = merged // channels
    voxels = slab_depth * slab_rows * width_cells
    padded_list = []
    pre_list = []
    current = features
    for layer in range(layers):
        padded = with_halo(current, (("depth", 0), ("row", 1)), 1)
        padded_list.append(padded)
        pre_full = convolve(padded, conv_weights[0, layer])
        pre_list.append(pre_full.astype(jnp.bfloat16))
        current = jax.nn.silu(pre_full).astype(jnp.bfloat16)
    hidden = current.reshape(voxels, channels)
    probs = softmax_rows(hidden, head_weights[0])
    own_peer = lax.axis_index("peer")
    partner = lax.dynamic_index_in_dim(matching, own_peer, 1, keepdims=False)
    own_probs = probs.astype(jnp.bfloat16).reshape(slab_depth, slab_rows, width_cells * classes)
    piece = lax.all_gather(own_probs[None], "peer", axis=0, tiled=True)
    owners = jnp.arange(piece.shape[0], dtype=jnp.int32)
    chosen = (owners[:, None] == partner[None, :]).astype(jnp.bfloat16)
    partner_probs = jnp.einsum("pd,pdrx->drx", chosen, piece, preferred_element_type=jnp.float32)
    partner_flat = partner_probs.reshape(voxels, classes)
    onehot = (labels.reshape(voxels, 1) == jnp.arange(classes, dtype=jnp.int32)[None, :]).astype(
        jnp.float32
    )
    mixed_grad = probs - 0.5 * onehot - 0.5 * partner_flat
    head_part = lax.dot_general(
        hidden,
        mixed_grad,
        (((0,), (0,)), ((), ())),
        precision=lax.Precision.HIGHEST,
        preferred_element_type=jnp.float32,
    )
    back_hidden = jnp.dot(
        mixed_grad, head_weights[0].astype(jnp.float32).T, precision=lax.Precision.HIGHEST
    )
    last_slope = slope(pre_list[layers - 1]).reshape(voxels, channels)
    grad_pre = (
        (back_hidden * last_slope).astype(jnp.bfloat16).reshape(slab_depth, slab_rows, merged)
    )
    kernel_grads = [None] * layers
    input_grad = None
    for layer in reversed(range(layers)):
        partial_grad = weight_grad(padded_list[layer], grad_pre, channels)
        kernel_grads[layer] = partial_grad
        padded_grad = with_halo(grad_pre, (("depth", 0), ("row", 1)), 1)
        back_input = convolve(padded_grad, flipped(conv_weights[0, layer]))
        if layer > 0:
            grad_pre = (back_input * slope(pre_list[layer - 1])).astype(jnp.bfloat16)
        else:
            input_grad = back_input.astype(jnp.bfloat16)
    stacked = jnp.stack(kernel_grads)
    head_total, stacked = (
        lax.psum(head_part.astype(jnp.bfloat16), ("depth", "row")).astype(jnp.float32),
        lax.psum(stacked.astype(jnp.bfloat16), ("depth", "row")).astype(jnp.float32),
    )
    return (stacked[None], head_total[None], input_grad[None])


def solution(mesh):
    placed = (
        P("depth", "row", None),
        P("depth", "row", None),
        P("peer", None, None, None),
        P("peer", None, None),
        P("depth", None),
    )
    return jax.shard_map(
        body,
        mesh=mesh,
        in_specs=placed,
        out_specs=(
            P("peer", None, None, None),
            P("peer", None, None),
            P("peer", "depth", "row", None),
        ),
        check_vma=False,
    )
```

profile of v0, /device:TPU:1, one launch (start us, length us, event | category | flops | bytes accessed | tf_op | source)
XLA Modules:
  0.0 995.5 jit_solution(811893436756225199)
XLA Ops:
  8.0 4.3 collective-permute-start
  17.3 5.0 collective-permute-start.2
  29.4 32.4 %while.124 = (s32[]{:T(128)}, f32[3,512,32]{1,2,0:T(8,128)}, s32[3]{0:T(128)S(1)}, bf16[5,10,66,32]{3,2,1,0:T(8,128)(2,1)S(1)}, bf16[864,32]{1,0:T(8,128)(2,1)},...) while((s32[]{:T(128)}, f32[3,512,32]{1,2,0:T(8,128)}, s32[3]{0:T(128)S(1)}, ...), condition=%wide.region_1.2_spmd, body=%wide.region_0.1_spmd.sunk | while | flops 28311560 | bytes 4710627 | solution.py:54
  33.9 4.3 concatenate.884
  83.4 32.4 %while.125 = (s32[]{:T(128)}, f32[3,512,32]{1,2,0:T(8,128)}, s32[3]{0:T(128)S(1)}, bf16[5,10,66,32]{3,2,1,0:T(8,128)(2,1)S(1)}, bf16[864,32]{1,0:T(8,128)(2,1)},...) while((s32[]{:T(128)}, f32[3,512,32]{1,2,0:T(8,128)}, s32[3]{0:T(128)S(1)}, ...), condition=%wide.region_3.4_spmd, body=%wide.region_2.3_spmd.sunk | while | flops 28311560 | bytes 4710627 | solution.py:54
  136.5 33.5 %while.126 = (s32[]{:T(128)}, f32[3,512,32]{1,2,0:T(8,128)}, s32[3]{0:T(128)}, bf16[5,10,66,32]{3,2,1,0:T(8,128)(2,1)S(1)}, bf16[864,32]{1,0:T(8,128)(2,1)}, /*index=5*/s32[]{:T(128)}, s32[]{:T(128)}, s32[]{:T(128)}, s32[]{}, s32[]{}) while((s32[]{:T(128)}, f32[3,512,32]{1,2,0:T(8,128)}, s32[3]{0:T(128)}, ...), condition=%wide.region_5.6_spmd, body=%wide.region_4.5_spmd.sunk | while | flops 28311560 | bytes 4710627 | solution.py:54
  190.9 34.5 %while.127 = (s32[]{:T(128)}, f32[3,512,32]{1,2,0:T(8,128)}, s32[3]{0:T(128)S(1)}, bf16[5,10,66,32]{3,2,1,0:T(8,128)(2,1)S(1)}, bf16[864,32]{1,0:T(8,128)(2,1)},...) while((s32[]{:T(128)}, f32[3,512,32]{1,2,0:T(8,128)}, s32[3]{0:T(128)S(1)}, ...), condition=%wide.region_7.8_spmd, body=%wide.region_6.7_spmd.sunk | while | flops 28311560 | bytes 4743395 | solution.py:54
  195.6 4.6 concatenate.887
  207.1 4.6 concatenate.887
  218.6 4.6 concatenate.887
  245.1 68.0 %all-gather.2.cloned.1.call-done = bf16[8,3,8,6656]{3,2,1,0:T(8,128)(2,1)} async-done(((bf16[1,3,8,6656]{3,2,1,0:T(8,128)(2,1)}), bf16[8,3,8,6656]{3,2,1,0:T(8,128)(2,1)}) %all-gather.2.cloned.1.call-update) | async-done | bytes 2555920 | tf_op jit(solution)/shard_map/all_gather | solution.py:121
  329.9 4.6 collective-permute-start.16
  334.5 36.3 %while.135 = (s32[]{:T(128)}, f32[864,32]{0,1:T(8,128)S(1)}, s32[3]{0:T(128)S(1)}, bf16[5,10,66,32]{3,2,1,0:T(8,128)(2,1)S(1)}, bf16[3,512,32]{2,1,0:T(8,128)(2,...) while((s32[]{:T(128)}, f32[864,32]{0,1:T(8,128)S(1)}, ...), condition=%wide.region_22.23_spmd.clone, body=%wide.region_21.22_spmd.clone.sunk | while | flops 28366860 | bytes 4808974 | solution.py:75
  340.4 4.7 concatenate.895
  352.5 4.7 concatenate.895
  364.6 4.7 concatenate.895
  373.9 5.6 collective-permute-start.18
  383.3 65.4 %psum.15 = bf16[1,32,104]{2,1,0:T(8,128)(2,1)S(1)} all-reduce(bf16[1,32,104]{2,1,0:T(8,128)(2,1)S(1)} %fusion.23), channel_id=1, replica_groups=mesh['peer'=8,'depth'=4,'row'=8] {'depth','row'}, use_global_device_ids=true, to_apply=%region_24.25 | all-reduce | flops 3328 | bytes 13312 | tf_op jit(solution)/shard_map/psum | solution.py:157
  453.2 34.6 %while.128 = (s32[]{:T(128)}, f32[3,512,32]{1,2,0:T(8,128)}, s32[3]{0:T(128)S(1)}, bf16[5,10,66,32]{3,2,1,0:T(8,128)(2,1)S(1)}, bf16[864,32]{1,0:T(8,128)(2,1)},...) while((s32[]{:T(128)}, f32[3,512,32]{1,2,0:T(8,128)}, s32[3]{0:T(128)S(1)}, ...), condition=%wide.region_10.11_spmd, body=%wide.region_9.10_spmd.sunk | while | flops 28311560 | bytes 4743395 | solution.py:54
  457.8 4.6 concatenate.888
  469.4 4.6 concatenate.888
  480.9 4.6 concatenate.888
  495.3 35.1 %while.134 = (s32[]{:T(128)}, f32[864,32]{0,1:T(8,128)}, s32[3]{0:T(128)S(1)}, bf16[5,10,66,32]{3,2,1,0:T(8,128)(2,1)S(1)}, bf16[3,512,32]{1,2,0:T(8,128)(2,1)},...) while((s32[]{:T(128)}, f32[864,32]{0,1:T(8,128)}, ...), condition=%wide.region_20.21_spmd.clone, body=%wide.region_19.20_spmd.clone.sunk | while | flops 28366860 | bytes 4681998 | solution.py:75
  533.4 4.8 collective-permute-start.23
  542.5 31.8 %while.129 = (s32[]{:T(128)}, f32[3,512,32]{1,2,0:T(8,128)}, s32[3]{0:T(128)S(1)}, bf16[5,10,66,32]{3,2,1,0:T(8,128)(2,1)S(1)}, bf16[864,32]{1,0:T(8,128)(2,1)},...) while((s32[]{:T(128)}, f32[3,512,32]{1,2,0:T(8,128)}, s32[3]{0:T(128)S(1)}, ...), condition=%wide.region_12.13_spmd, body=%wide.region_11.12_spmd.sunk | while | flops 28311560 | bytes 4710627 | solution.py:54
  592.0 35.8 %while.133 = (s32[]{:T(128)}, f32[864,32]{0,1:T(8,128)}, s32[3]{0:T(128)S(1)}, bf16[5,10,66,32]{3,2,1,0:T(8,128)(2,1)S(1)}, bf16[3,512,32]{1,2,0:T(8,128)(2,1)},...) while((s32[]{:T(128)}, f32[864,32]{0,1:T(8,128)}, ...), condition=%wide.region_18.19_spmd.clone, body=%wide.region_17.18_spmd.clone.sunk | while | flops 28366860 | bytes 4681998 | solution.py:75
  630.5 32.0 %while.130 = (s32[]{:T(128)}, f32[3,512,32]{1,2,0:T(8,128)}, s32[3]{0:T(128)S(1)}, bf16[5,10,66,32]{3,2,1,0:T(8,128)(2,1)S(1)}, bf16[864,32]{1,0:T(8,128)(2,1)},...) while((s32[]{:T(128)}, f32[3,512,32]{1,2,0:T(8,128)}, s32[3]{0:T(128)S(1)}, ...), condition=%wide.region_14.15_spmd, body=%wide.region_13.14_spmd.sunk | while | flops 28311560 | bytes 4710627 | solution.py:54
  666.3 35.8 %while.132 = (s32[]{:T(128)}, f32[864,32]{0,1:T(8,128)}, s32[3]{0:T(128)S(1)}, bf16[5,10,66,32]{3,2,1,0:T(8,128)(2,1)S(1)}, bf16[3,512,32]{1,2,0:T(8,128)(2,1)},...) while((s32[]{:T(128)}, f32[864,32]{0,1:T(8,128)}, ...), condition=%wide.region_16.17_spmd.clone, body=%wide.region_15.16_spmd.clone.sunk | while | flops 28366860 | bytes 4681998 | solution.py:75
  722.1 32.5 %while.131 = (s32[]{:T(128)}, bf16[3,512,32]{1,2,0:T(8,128)(2,1)}, s32[3]{0:T(128)S(1)}, bf16[5,10,66,32]{3,2,1,0:T(8,128)(2,1)S(1)}, bf16[864,32]{1,0:T(8,128)(...) while((s32[]{:T(128)}, bf16[3,512,32]{1,2,0:T(8,128)(2,1)}, s32[3]{0:T(128)S(1)}, ...), condition=%wide.region_26.27_spmd, body=%wide.region_25.26_spmd.sunk | while | flops 28311560 | bytes 4710627 | solution.py:54
  726.6 4.3 concatenate.891
  737.5 4.3 concatenate.891
  756.7 230.0 %all-reduce.10.cloned.1.call-done = bf16[1,4,864,32]{2,3,1,0:T(8,128)(2,1)} async-done(((bf16[1,4,864,32]{2,3,1,0:T(8,128)(2,1)}), bf16[1,4,864,32]{2,3,1,0:T(8,128)(2,1)}) %all-reduce.10.cloned.1.call-update) | async-done | bytes 221200 | tf_op jit(solution)/shard_map/psum | solution.py:158
  (389 shorter events, 451.9 us)
Async XLA Ops:
  7.2 306.0 %all-gather.2.cloned.1.call-start = ((), (), s32[]{:S(2)}) async-start(), calls=%async_computation | async-start | bytes 2875392 | tf_op jit(solution)/shard_map/all_gather | solution.py:121
  8.0 5.7 collective-permute-start
  12.4 4.8 collective-permute-start.1
  17.3 9.3 collective-permute-start.2
  22.3 5.3 collective-permute-start.3
  63.7 4.9 collective-permute-start.4
  67.2 4.8 collective-permute-start.5
  72.1 6.9 collective-permute-start.6
  76.3 5.3 collective-permute-start.7
  117.5 4.7 collective-permute-start.8
  120.8 4.7 collective-permute-start.9
  125.6 6.3 collective-permute-start.10
  128.9 5.3 collective-permute-start.11
  173.6 4.7 collective-permute-start.13
  178.3 6.3 collective-permute-start.14
  181.8 5.3 collective-permute-start.15
  232.7 754.0 %all-reduce.10.cloned.1.call-start = ((), (), s32[]{:S(2)}) async-start(), calls=%async_computation.1 | async-start | bytes 458752 | tf_op jit(solution)/shard_map/psum | solution.py:158
  327.7 45.4 %collective-permute-start.17 = (bf16[1,8,2048]{2,1,0:T(8,128)(2,1)}, bf16[1,8,2048]{2,1,0:T(8,128)(2,1)}, u32[]{:S(2)}, u32[]{:S(2)}) collective-permute-start(bf16[1,8,2048]{2,1,0:T(8,128)(2,1)} %slice.1113), channel_id=1, source_target_pairs={{8,0},{16,8},{24,16},{9,1},{17,9},{25,17},{10,2},{18,10},{26,18},{... | collective-permute-start | bytes 98312 | tf_op jit(solution)/shard_map/ppermute | solution.py:17
  329.9 42.4 %collective-permute-start.16 = (bf16[1,8,2048]{2,1,0:T(8,128)(2,1)}, bf16[1,8,2048]{2,1,0:T(8,128)(2,1)}, u32[]{:S(2)}, u32[]{:S(2)}) collective-permute-start(bf16[1,8,2048]{2,1,0:T(8,128)(2,1)} %slice.1111), channel_id=1, source_target_pairs={{0,8},{8,16},{16,24},{1,9},{9,17},{17,25},{2,10},{10,18},{18,26},{... | collective-permute-start | bytes 98312 | tf_op jit(solution)/shard_map/ppermute | solution.py:15
  373.9 75.5 %collective-permute-start.18 = (bf16[5,1,2048]{2,1,0:T(2,128)(2,1)S(1)}, bf16[5,1,2048]{2,1,0:T(2,128)(2,1)S(1)}, u32[]{:S(2)}, u32[]{:S(2)}) collective-permute-start(bf16[5,1,2048]{2,1,0:T(2,128)(2,1)S(1)} %get-tuple-element.920), channel_id=1, source_target_pairs={{0,1},{1,2},{2,3},{3,4},{4,5},{5,6},{6,7},{8,9},{9,10},{10,11},{11... | collective-permute-start | bytes 61448 | tf_op jit(solution)/shard_map/ppermute | solution.py:15
  379.5 69.9 %collective-permute-start.19 = (bf16[5,1,2048]{2,1,0:T(2,128)(2,1)S(1)}, bf16[5,1,2048]{2,1,0:T(2,128)(2,1)S(1)}, u32[]{:S(2)}, u32[]{:S(2)}) collective-permute-start(bf16[5,1,2048]{2,1,0:T(2,128)(2,1)S(1)} %get-tuple-element.921), channel_id=1, source_target_pairs={{1,0},{2,1},{3,2},{4,3},{5,4},{6,5},{7,6},{9,8},{10,9},{11,10},{12... | collective-permute-start | bytes 61448 | tf_op jit(solution)/shard_map/ppermute | solution.py:17
  491.9 38.5 %collective-permute-start.20 = (bf16[1,8,2048]{2,1,0:T(8,128)(2,1)}, bf16[1,8,2048]{2,1,0:T(8,128)(2,1)}, u32[]{:S(2)}, u32[]{:S(2)}) collective-permute-start(bf16[1,8,2048]{2,1,0:T(8,128)(2,1)} %get-tuple-element.934), channel_id=1, source_target_pairs={{0,8},{8,16},{16,24},{1,9},{9,17},{17,25},{2,10},{10,18},{18,26},{... | collective-permute-start | bytes 98312 | tf_op jit(solution)/shard_map/ppermute | solution.py:15
  493.8 36.6 %collective-permute-start.21 = (bf16[1,8,2048]{2,1,0:T(8,128)(2,1)}, bf16[1,8,2048]{2,1,0:T(8,128)(2,1)}, u32[]{:S(2)}, u32[]{:S(2)}) collective-permute-start(bf16[1,8,2048]{2,1,0:T(8,128)(2,1)} %get-tuple-element.935), channel_id=1, source_target_pairs={{8,0},{16,8},{24,16},{9,1},{17,9},{25,17},{10,2},{18,10},{26,18},{... | collective-permute-start | bytes 98312 | tf_op jit(solution)/shard_map/ppermute | solution.py:17
  531.5 8.4 collective-permute-start.22
  533.4 6.4 collective-permute-start.23
  577.1 6.3 collective-permute-start.24
  581.3 5.0 collective-permute-start.25
  587.0 40.8 %collective-permute-start.26 = (bf16[5,1,2048]{2,1,0:T(2,128)(2,1)}, bf16[5,1,2048]{2,1,0:T(2,128)(2,1)}, u32[]{:S(2)}, u32[]{:S(2)}) collective-permute-start(bf16[5,1,2048]{2,1,0:T(2,128)(2,1)} %get-tuple-element.916), channel_id=1, source_target_pairs={{0,1},{1,2},{2,3},{3,4},{4,5},{5,6},{6,7},{8,9},{9,10},{10,11},{11... | collective-permute-start | bytes 61448 | tf_op jit(solution)/shard_map/ppermute | solution.py:15
  588.9 38.9 %collective-permute-start.27 = (bf16[5,1,2048]{2,1,0:T(2,128)(2,1)}, bf16[5,1,2048]{2,1,0:T(2,128)(2,1)}, u32[]{:S(2)}, u32[]{:S(2)}) collective-permute-start(bf16[5,1,2048]{2,1,0:T(2,128)(2,1)} %get-tuple-element.917), channel_id=1, source_target_pairs={{1,0},{2,1},{3,2},{4,3},{5,4},{6,5},{7,6},{9,8},{10,9},{11,10},{12... | collective-permute-start | bytes 61448 | tf_op jit(solution)/shard_map/ppermute | solution.py:17
  706.9 5.2 collective-permute-start.29
  712.2 7.0 collective-permute-start.30
  715.7 5.3 collective-permute-start.31
  (32 other events, 850.4 us)
Sparse Core Ops, SparseCore 0:
  232.8 80.3 all-gather.1
  719.3 267.3 all-reduce.9
where the time goes:
time: 1020 us; the launch traced here: 995 us
  waiting for transfers between devices  327 us (32%)
  local copies, waits for them, and re-layouts  318 us (31%)
  loops' own time  85.7 us (8%)
  starting transfers between devices  85.6 us (8%)
  matrix products  76.3 us (7%)
  blocking collectives  65.4 us (6%)
  other arithmetic  22 us (2%)
  between operations  15.2 us (1%)
    psum x1, waiting for transfers between devices, body(): lax.psum(stacked.astype(jnp.bfloat16), ('depth', 'row')).astype(jnp.float32)  230 us
    concatenate x36, local copies, waits for them, and re-layouts, columns(): return jnp.concatenate(pieces, axis=-1).reshape(rows_out * width_out, -1)  156 us
    slice x36, local copies, waits for them, and re-layouts, columns(): block[depth_off, row_off:row_off + rows_out, col_off:col_off + width_out, :]  73.3 us
    all_gather x1, waiting for transfers between devices, body(): piece = lax.all_gather(own_probs[None], 'peer', axis=0, tiled=True)  68 us
    psum x1, blocking collectives, body(): lax.psum(head_part.astype(jnp.bfloat16), ('depth', 'row'))  65.4 us
    ppermute x16, starting transfers between devices, with_halo(): lax.ppermute(tail, axis, [(i, (i + 1) % count) for i in range(ends)])  55 us
    dot_general x24, matrix products, one_slice(): jnp.dot(columns(block, rows_out, width_out), weight, preferred_element_ty...  48.5 us
    another operation x8, loops' own time, convolve(): result = lax.map(one_slice, jnp.arange(depth_out, dtype=jnp.int32))  46.9 us
  transfers between devices with their start and end apart: 34, of which 13 were waited for; matrix products, arithmetic and copies ran while one was open for 14% of the time, Pallas kernels for 0%

commit v1 on v0

v1 whole, which is shorter than its diff:
```python
import functools

import jax
import jax.numpy as jnp
from jax import lax
from jax.experimental import pallas as pl
from jax.experimental.pallas import tpu as pltpu
from jax.sharding import PartitionSpec as P

MESH = pl.DeviceIdType.MESH
F32 = jnp.float32
BF16 = jnp.bfloat16
OFFSETS = [(i, j) for i in range(3) for j in range(3)]
NEIGHBOURS = [(0, 1), (0, -1), (1, 0), (-1, 0), (1, 1), (1, -1), (-1, 1), (-1, -1)]


def nt(a, b):
    return lax.dot_general(a, b, (((1,), (1,)), ((), ())), preferred_element_type=F32)


def nn(a, b):
    return lax.dot_general(a, b, (((1,), (0,)), ((), ())), preferred_element_type=F32)


def slope(pre):
    s = 1.0 / (1.0 + jnp.exp(-pre))
    return s * (1.0 + pre * (1.0 - s))


def kernel(
    sizes,
    x_ref, lab_ref, w_ref, head_ref, match_ref,
    cg_ref, hg_ref, ig_ref,
    xe, ge, wt, wpad, tmp, slp, hcat, tcat, hd, hzin, hzout, hall, zin, zout, part,
    pk, rsin, dep, fin,
    halo_s, halo_r, hx_s, hx_r, ax_s, ax_r, z_s, z_r, rs_s, rs_r, dp_s, dp_r, ag_s, ag_r,
):
    nx, nd, nr, slab, rows, classes, layers = sizes
    cells = slab * rows * 16
    peer = lax.axis_index("peer")
    depth = lax.axis_index("depth")
    row = lax.axis_index("row")
    xpos, zhalf = lax.div(peer, 2), lax.rem(peer, 2)
    zpos = zhalf * nd + depth

    def near(dp, dr):
        where = {}
        if dr:
            where["row"] = lax.rem(row + dr + nr, nr)
        if dp:
            z = lax.rem(zpos + dp + 2 * nd, 2 * nd)
            where["peer"] = 2 * xpos + lax.div(z, nd)
            where["depth"] = lax.rem(z, nd)
        return where

    def x_mate(s):
        return {"peer": 2 * lax.rem(xpos + s, nx) + zhalf}

    z_mate = {"peer": 2 * xpos + (1 - zhalf)}

    def row_mate(s):
        return {"row": lax.rem(row + s, nr)}

    def depth_mate(s):
        return {"depth": lax.rem(depth + s, nd)}

    xe[...] = jnp.zeros_like(xe)
    ge[...] = jnp.zeros_like(ge)
    mates = [near(*step) for step in NEIGHBOURS]
    mates += [x_mate(s) for s in range(1, nx)] + [z_mate]
    mates += [row_mate(s) for s in range(2, nr - 1)]
    mates += [depth_mate(s) for s in range(1, nd)]
    barrier = pltpu.get_barrier_semaphore()
    for mate in mates:
        pl.semaphore_signal(barrier, inc=1, device_id=mate, device_id_type=MESH)

    started = []

    def remote(src, dst, send, recv, mate):
        copy = pltpu.make_async_remote_copy(
            src_ref=src, dst_ref=dst, send_sem=send, recv_sem=recv, device_id=mate, device_id_type=MESH
        )
        return copy

    for d in range(slab):
        for b in range(16):
            tmp[pl.ds(d * rows * 16 + b, rows, stride=16), :] = x_ref[d, :, b * 128 : (b + 1) * 128].astype(F32)
    xe[0, 1 : slab + 1, 1 : rows + 1] = tmp[...].reshape(slab, rows, 16, 128).astype(BF16)

    hcat[...] = jnp.zeros_like(hcat)
    tcat[...] = jnp.zeros_like(tcat)
    tmp[0:32, :] = jnp.zeros((32, 128), F32)
    tmp[0:32, 0:classes] = head_ref[...].astype(F32)
    head = tmp[0:32, :].astype(BF16)
    hd[xpos] = head
    for a in range(4):
        hcat[a * 32 : (a + 1) * 32, a * 128 : (a + 1) * 128] = head

    pl.semaphore_wait(barrier, len(mates))

    def halo_copies(buf, layer, ex):
        copies = []
        for n, (dp, dr) in enumerate(NEIGHBOURS):
            if dp == 0:
                src_p, dst_p = pl.ds(1, slab), pl.ds(1, slab)
            elif dp == 1:
                src_p = pl.ds(slab, 1)
                dst_p = pl.ds(jnp.where(depth == nd - 1, slab + 2, 0), 1)
            else:
                src_p = pl.ds(1, 1)
                dst_p = pl.ds(jnp.where(depth == 0, slab + 3, slab + 1), 1)
            if dr == 0:
                src_r, dst_r = pl.ds(1, rows), pl.ds(1, rows)
            elif dr == 1:
                src_r = pl.ds(rows, 1)
                dst_r = pl.ds(jnp.where(row == nr - 1, rows + 2, 0), 1)
            else:
                src_r = pl.ds(1, 1)
                dst_r = pl.ds(jnp.where(row == 0, rows + 3, rows + 1), 1)
            copies.append(
                remote(
                    buf.at[layer, src_p, src_r], buf.at[layer, dst_p, dst_r],
                    halo_s.at[ex, n], halo_r.at[ex, n], near(dp, dr),
                )
            )
        return copies

    def start(copies):
        for copy in copies:
            copy.start()
        started.extend(copies)
        return copies

    def arrive(copies):
        for copy in copies:
            copy.wait_recv()

    halo = start(halo_copies(xe, 0, 0))
    head_x = start(
        [remote(hd.at[xpos], hd.at[xpos], hx_s.at[s], hx_r.at[s], x_mate(s)) for s in range(1, nx)]
    )

    lane = lax.broadcasted_iota(jnp.int32, (cells, 128), 1)
    block = lax.rem(lax.broadcasted_iota(jnp.int32, (cells, 128), 0), 16)
    low = lane < 64
    inside = jnp.where(low, block, 15 - block) > 0

    def spill(y):
        e = y[:, 128:]
        moved = jnp.where(low, pltpu.roll(e, 1, 0), pltpu.roll(e, cells - 1, 0))
        return y[:, :128] + jnp.where(inside, moved, 0.0)

    wpad[:, 0 : 27 * 32] = w_ref[...].reshape(layers * 32, 27 * 32).astype(F32)
    wt[:, 1, 1:3] = jnp.zeros((9, 2, layers * 32, 128), BF16)
    group = lax.div(lax.broadcasted_iota(jnp.int32, (layers * 32, 128), 1), 32)

    def rolled(v, groups):
        shift = (groups * 32) % 128
        return v if shift == 0 else pltpu.roll(v, shift, 1)

    for ij in range(9):
        blk = None
        for k in range(3):
            t, g = divmod(3 * ij + k, 4)
            piece = rolled(wpad[:, t * 128 : (t + 1) * 128], k - g)
            blk = piece if blk is None else jnp.where(group == k, piece, blk)
        r0 = rolled(blk, -1)
        wt[ij, 0, 0] = jnp.where(group < 2, r0, 0.0).astype(BF16)
        wt[ij, 1, 0] = jnp.where(group == 3, r0, 0.0).astype(BF16)
        wt[ij, 0, 1] = jnp.where(group < 3, blk, 0.0).astype(BF16)
        wt[ij, 0, 2] = jnp.where(group > 0, rolled(blk, 1), 0.0).astype(BF16)
        r3 = rolled(blk, 2)
        wt[ij, 0, 3] = jnp.where(group > 1, r3, 0.0).astype(BF16)
        wt[ij, 1, 3] = jnp.where(group == 0, r3, 0.0).astype(BF16)

    def window(buf, layer, i, j):
        return buf[layer, i : i + slab, j : j + rows].reshape(cells, 128)

    def weights(layer, ij, half):
        return wt[ij, half, :, layer * 32 : (layer + 1) * 32, :].reshape(128, 128)

    def forward(layer):
        cols = jnp.concatenate([window(xe, layer, i, j) for i, j in OFFSETS], axis=1)
        band = jnp.concatenate(
            [jnp.concatenate([weights(layer, ij, 0), weights(layer, ij, 1)], axis=0) for ij in range(9)], axis=1
        )
        return spill(nt(cols, band))

    def backward(layer):
        cols = jnp.concatenate([window(ge, layer, 2 - i, 2 - j) for i, j in OFFSETS], axis=1)
        band = jnp.concatenate(
            [jnp.concatenate([weights(layer, ij, 0), weights(layer, ij, 1)], axis=1) for ij in range(9)], axis=0
        )
        return spill(nn(cols, band))

    for layer in range(layers):
        arrive(halo)
        y = forward(layer)
        act = (y / (1.0 + jnp.exp(-y))).astype(BF16)
        if layer + 1 < layers:
            xe[layer + 1, 1 : slab + 1, 1 : rows + 1] = act.reshape(slab, rows, 16, 128)
            halo = start(halo_copies(xe, layer + 1, layer + 1))
        else:
            hall[xpos] = act.reshape(slab, rows * 16, 128)
            act_x = start(
                [remote(hall.at[xpos], hall.at[xpos], ax_s.at[s], ax_r.at[s], x_mate(s)) for s in range(1, nx)]
            )
        slp[layer] = slope(y.astype(BF16).astype(F32))
        if layer == 1:
            arrive(head_x)
            for d in range(slab):
                hzout[d] = hd[lax.div(match_ref[d, 2 * xpos + (1 - zhalf)], 2)]
            head_z = start([remote(hzout, hzin, z_s.at[0], z_r.at[0], z_mate)])

    hidden = act

    col_class = lax.broadcasted_iota(jnp.int32, (rows * 16, 128), 1)
    real = col_class < classes
    spread_r = lax.broadcasted_iota(jnp.int32, (cells, slab * rows), 0)
    spread_c = lax.broadcasted_iota(jnp.int32, (cells, slab * rows), 1)
    spread = jnp.where(lax.div(spread_r, 16) == spread_c, 1.0, 0.0).astype(BF16)
    lab = nn(spread, lab_ref[...].reshape(slab * rows, 64).astype(F32).astype(BF16))
    vox = lax.broadcasted_iota(jnp.int32, (cells, 64), 1)
    own = lax.rem(lax.broadcasted_iota(jnp.int32, (cells, 64), 0), 16)
    lab = jnp.where(lax.div(vox, 4) == own, lab, 0.0).astype(BF16)
    pick_r = lax.broadcasted_iota(jnp.int32, (64, 512), 0)
    pick_c = lax.broadcasted_iota(jnp.int32, (64, 512), 1)
    pick = jnp.where(lax.rem(pick_r, 4) == lax.div(pick_c, 128), 1.0, 0.0).astype(BF16)
    class_of = nn(lab, pick)

    def softmax(act_plane, heads):
        logits = nn(act_plane, heads)
        out = []
        for a in range(4):
            ex = jnp.where(real, jnp.exp(logits[:, a * 128 : (a + 1) * 128]), 0.0)
            out.append(ex / jnp.sum(ex, axis=1, keepdims=True))
        return out

    n = rows * 16
    col_f = col_class.astype(F32)
    for d in range(slab):
        probs = softmax(hidden[d * n : (d + 1) * n], hcat[...])
        for a in range(4):
            mark = jnp.where(class_of[d * n : (d + 1) * n, a * 128 : (a + 1) * 128] == col_f, 0.5, 0.0)
            part[d, :, a * 128 : (a + 1) * 128] = probs[a] - mark

    arrive(act_x)
    for d in range(slab):
        zout[d] = hall[lax.div(match_ref[d, 2 * xpos + (1 - zhalf)], 2), d]
    act_z = start([remote(zout, zin, z_s.at[1], z_r.at[1], z_mate)])
    arrive(head_z)
    arrive(act_z)
    grad_rows = []
    for d in range(slab):
        source = match_ref[d, peer]
        near_half = lax.rem(source, 2) == zhalf
        mine = lax.div(source, 2)
        target_head = jnp.where(near_half, hd[mine].astype(F32), hzin[d].astype(F32)).astype(BF16)
        target_act = jnp.where(near_half, hall[mine, d].astype(F32), zin[d].astype(F32)).astype(BF16)
        for a in range(4):
            tcat[d, a * 32 : (a + 1) * 32, a * 128 : (a + 1) * 128] = target_head
        target = softmax(target_act, tcat[d])
        grad_rows.append(
            jnp.concatenate(
                [
                    (part[d, :, a * 128 : (a + 1) * 128] - 0.5 * target[a].astype(BF16).astype(F32)).astype(BF16)
                    for a in range(4)
                ],
                axis=1,
            )
        )
    dlogits = jnp.concatenate(grad_rows, axis=0)
    g = nt(dlogits, hcat[...]) * slp[layers - 1]

    group32 = lax.div(lax.broadcasted_iota(jnp.int32, (32, 128), 1), 32)
    group288 = lax.div(lax.broadcasted_iota(jnp.int32, (288, 128), 1), 32)
    own_chunks = 8 // nr

    def weight_grad(layer, g):
        left = jnp.where(low, pltpu.roll(g, cells - 1, 0), pltpu.roll(g, 1, 0))
        ok = jnp.where(low, 15 - block, block) > 0
        edge = jnp.where((lane < 32) | (lane >= 96), jnp.where(ok, left, 0.0), 0.0)
        both = jnp.concatenate([g, edge], axis=1).astype(BF16).T
        cols = jnp.concatenate([window(xe, layer, i, j) for i, j in OFFSETS], axis=1)
        prod = nn(both, cols)

        def take(at):
            return jnp.concatenate([prod[at : at + 32, ij * 128 : (ij + 1) * 128] for ij in range(9)], axis=0)

        s0 = jnp.where(group288 == 3, take(128), take(0))
        s3 = jnp.where(group288 == 0, take(224), take(96))
        total = take(32) + pltpu.roll(s0, 32, 1) + pltpu.roll(take(64), 96, 1) + pltpu.roll(s3, 64, 1)
        for t in range(7):
            tile = None
            ks = [(gr, *divmod(4 * t + gr, 3)) for gr in range(4) if 4 * t + gr < 27]
            for ij in sorted({ij for _, ij, _ in ks}):
                mine = [(gr, k) for gr, at, k in ks if at == ij]
                moved = rolled(total[ij * 32 : (ij + 1) * 32], mine[0][0] - mine[0][1])
                tile = moved if tile is None else jnp.where(group32 >= mine[0][0], moved, tile)
            pk[layer, t // own_chunks, t % own_chunks] = tile.astype(BF16)

    def send_row(layer):
        return start(
            [
                remote(
                    pk.at[layer, lax.rem(row + s, nr)], rsin.at[layer, s], rs_s.at[layer, s], rs_r.at[layer, s], row_mate(s)
                )
                for s in range(1, nr)
            ]
        )

    def send_depth(layer, copies):
        arrive(copies)
        total = pk[layer, row].astype(F32)
        for s in range(1, nr):
            total = total + rsin[layer, s].astype(F32)
        dep[layer, depth] = total.astype(BF16)
        return start(
            [
                remote(
                    dep.at[layer, depth], dep.at[layer, depth], dp_s.at[layer, s], dp_r.at[layer, s], depth_mate(s)
                )
                for s in range(1, nd)
            ]
        )

    def send_all(layer, copies):
        arrive(copies)
        total = dep[layer, 0].astype(F32)
        for s in range(1, nd):
            total = total + dep[layer, s].astype(F32)
        fin[layer, row] = total.astype(BF16)
        return start(
            [
                remote(fin.at[layer, row], fin.at[layer, row], ag_s.at[layer, s], ag_r.at[layer, s], row_mate(s))
                for s in range(1, nr)
            ]
        )

    def finish(layer, copies):
        arrive(copies)
        for t in range(7):
            wide = min(128, 27 * 32 - t * 128)
            cg_ref[layer, :, t * 128 : t * 128 + wide] = fin[layer, t // own_chunks, t % own_chunks].astype(F32)[:, :wide]
        if layer == layers - 1:
            hg_ref[...] = fin[layer, 7 // own_chunks, 7 % own_chunks].astype(F32)[:, :classes]

    stage = {}
    for layer in reversed(range(layers)):
        ge[layer, 1 : slab + 1, 1 : rows + 1] = g.astype(BF16).reshape(slab, rows, 16, 128)
        halo = start(halo_copies(ge, layer, layers + layer))
        if layer == layers - 1:
            wide = nn(hidden.T, dlogits)
            heads = wide[0:32, 0:128]
            for a in range(1, 4):
                heads = heads + wide[a * 32 : (a + 1) * 32, a * 128 : (a + 1) * 128]
            pk[layer, 7 // own_chunks, 7 % own_chunks] = heads.astype(BF16)
        else:
            pk[layer, 7 // own_chunks, 7 % own_chunks] = jnp.zeros((32, 128), BF16)
        weight_grad(layer, g)
        stage[layer] = send_row(layer)
        if layer + 1 < layers:
            stage[layer + 1] = send_depth(layer + 1, stage[layer + 1])
        if layer + 2 < layers:
            stage[layer + 2] = send_all(layer + 2, stage[layer + 2])
        if layer + 3 < layers:
            finish(layer + 3, stage[layer + 3])
        arrive(halo)
        back = backward(layer)
        if layer > 0:
            g = back * slp[layer - 1]
    stage[0] = send_depth(0, stage[0])
    stage[1] = send_all(1, stage[1])
    finish(2, stage[2])
    tmp[...] = back
    for d in range(slab):
        for b in range(16):
            ig_ref[d, :, b * 128 : (b + 1) * 128] = tmp[pl.ds(d * rows * 16 + b, rows, stride=16), :].astype(BF16)
    stage[0] = send_all(0, stage[0])
    finish(1, stage[1])
    finish(0, stage[0])
    for copy in started:
        copy.wait_send()


def solution(mesh):
    np_, nd, nr = mesh.shape["peer"], mesh.shape["depth"], mesh.shape["row"]
    nx = np_ // 2

    def body(features, labels, conv_weights, head_weights, matching):
        slab, rows, merged = features.shape
        layers = conv_weights.shape[1]
        classes = head_weights.shape[2]
        cells = slab * rows * 16
        chunk = (8 // nr, 32, 128)
        ext = (layers, slab + 4, rows + 4, 16, 128)
        vmem = pl.BlockSpec(memory_space=pltpu.VMEM)
        dma = pltpu.SemaphoreType.DMA
        scratch = [
            pltpu.VMEM(ext, BF16),
            pltpu.VMEM(ext, BF16),
            pltpu.VMEM((9, 2, 4, layers * 32, 128), BF16),
            pltpu.VMEM((layers * 32, 896), F32),
            pltpu.VMEM((cells, 128), F32),
            pltpu.VMEM((layers, cells, 128), F32),
            pltpu.VMEM((128, 512), BF16),
            pltpu.VMEM((slab, 128, 512), BF16),
            pltpu.VMEM((nx, 32, 128), BF16),
            pltpu.VMEM((slab, 32, 128), BF16),
            pltpu.VMEM((slab, 32, 128), BF16),
            pltpu.VMEM((nx, slab, rows * 16, 128), BF16),
            pltpu.VMEM((slab, rows * 16, 128), BF16),
            pltpu.VMEM((slab, rows * 16, 128), BF16),
            pltpu.VMEM((slab, rows * 16, 512), F32),
            pltpu.VMEM((layers, nr) + chunk, BF16),
            pltpu.VMEM((layers, nr) + chunk, BF16),
            pltpu.VMEM((layers, nd) + chunk, BF16),
            pltpu.VMEM((layers, nr) + chunk, BF16),
            dma((2 * layers, 8)), dma((2 * layers, 8)),
            dma((nx,)), dma((nx,)),
            dma((nx,)), dma((nx,)),
            dma((2,)), dma((2,)),
            dma((layers, nr)), dma((layers, nr)),
            dma((layers, nd)), dma((layers, nd)),
            dma((layers, nr)), dma((layers, nr)),
        ]
        sizes = (nx, nd, nr, slab, rows, classes, layers)
        cg, hg, ig = pl.pallas_call(
            functools.partial(kernel, sizes),
            out_shape=(
                jax.ShapeDtypeStruct((layers, 32, 27 * 32), F32),
                jax.ShapeDtypeStruct((32, classes), F32),
                jax.ShapeDtypeStruct((slab, rows, merged), BF16),
            ),
            in_specs=[vmem, vmem, vmem, vmem, pl.BlockSpec(memory_space=pltpu.SMEM)],
            out_specs=(vmem, vmem, vmem),
            scratch_shapes=scratch,
            compiler_params=pltpu.CompilerParams(collective_id=0, has_side_effects=True),
        )(
            features,
            labels,
            conv_weights[0].transpose(0, 2, 1),
            head_weights[0],
            matching,
        )
        return cg.transpose(0, 2, 1)[None], hg[None], ig[None]

    return jax.shard_map(
        body,
        mesh=mesh,
        in_specs=(
            P("depth", "row", None),
            P("depth", "row", None),
            P("peer", None, None, None),
            P("peer", None, None),
            P("depth", None),
        ),
        out_specs=(
            P("peer", None, None, None),
            P("peer", None, None),
            P("peer", "depth", "row", None),
        ),
        check_vma=False,
    )
```

time: 1020 us -> 79.6 us (0.08); the launches traced: 995 us -> 79.5 us
  waiting for transfers between devices: 327 us -> 0 us
  local copies, waits for them, and re-layouts: 318 us -> 3.1 us
  loops' own time: 85.7 us -> 0 us
  starting transfers between devices: 85.6 us -> 0 us
  matrix products: 76.3 us -> 0 us
  Pallas kernels: 0 us -> 75.7 us
  blocking collectives: 65.4 us -> 0 us
  other arithmetic: 22 us -> 0 us
  between operations: 15.2 us -> 0.66 us
    psum x1 -> x0, waiting for transfers between devices: 230 us -> none  [body(): lax.psum(stacked.astype(jnp.bfloat16), ('depth', 'row')).astype(jnp.float32)]
    concatenate x38 -> x0, local copies, waits for them, and re-layouts: 157 us -> none  [the longest x36 156 us: columns(): return jnp.concatenate(pieces, axis=-1).reshape(rows_out * width_out, -1)]
    another operation x12 -> x0, loops' own time: 85.7 us -> none  [the longest x8 46.9 us: convolve(): result = lax.map(one_slice, jnp.arange(depth_out, dtype=jnp.int32))]
    ppermute x32 -> x0, starting transfers between devices: 85 us -> none  [the longest x16 55 us: with_halo(): lax.ppermute(tail, axis, [(i, (i + 1) % count) for i in range(ends)])]
    slice x51 -> x0, local copies, waits for them, and re-layouts: 78.3 us -> none  [the longest x36 73.3 us: columns(): block[depth_off, row_off:row_off + rows_out, col_off:col_off + width_out, :]]
    dot_general x40 -> x0, matrix products: 76.3 us -> none  [the longest x24 48.5 us: one_slice(): jnp.dot(columns(block, rows_out, width_out), weight, preferred_element_ty...]
    pallas_call x0 -> x1, Pallas kernels: none -> 75.7 us  [body(): pl.pallas_call(functools.partial(kernel, sizes), out_shape=(jax.ShapeDtyp...]
    all_gather x1 -> x0, waiting for transfers between devices: 68 us -> none  [body(): piece = lax.all_gather(own_probs[None], 'peer', axis=0, tiled=True)]
  transfers between devices with their start and end apart: 34 -> 0, of which waited for: 13 -> 0; matrix products, arithmetic and copies ran while one was open for 14% -> 0% of each run, Pallas kernels for 0% -> 0%
where the time goes in v1:
time: 79.6 us; the launch traced here: 79.5 us
  Pallas kernels  75.7 us (95%)
  local copies, waits for them, and re-layouts  3.1 us (4%)
    pallas_call x1, Pallas kernels, body(): pl.pallas_call(functools.partial(kernel, sizes), out_shape=(jax.ShapeDtyp...  75.7 us
    unnamed x7, local copies, waits for them, and re-layouts  3.1 us

profile of v1, /device:TPU:1, one launch (start us, length us, event | category | flops | bytes accessed | tf_op | source)
XLA Modules:
  0.0 79.5 jit_solution(16843488790248286452)
XLA Ops:
  0.6 75.7 %shard_map.76 = (f32[4,32,864]{2,1,0:T(8,128)}, f32[32,104]{1,0:T(8,128)}, bf16[3,8,2048]{2,1,0:T(8,128)(2,1)}) custom-call(bf16[3,8,2048]{2,1,0:T(8,128)(2,1)} %x_ref.1, s32[3,8,64]{2,1,0:T(8,128)} %lab_ref.1, bf16[4,32,864]{2,1,0:T(8,128)(2,1)} %bitcast.10, bf16[32,104]{1,0:T(8,128)(2,1)} %bitcast.13, s32[3,8]{1,0:T(4,128)} %match_ref.1), custom_call_target="tpu_custom_call" | custom-call | tf_op jit(solution)/shard_map/pallas_call | solution.py:428
  76.3 0.0 copy-start.1
  76.3 0.0 copy-start
  76.4 1.9 %copy.11 = f32[1,4,864,32]{2,3,1,0:T(8,128)} copy(f32[1,4,864,32]{2,3,1,0:T(8,128)} %bitcast.9) | data formatting | bytes 884736
  78.2 0.0 copy-done.1
  78.2 0.6 copy.12
  78.8 0.0 copy-done
  78.8 0.6 copy.13
Async XLA Ops:
  76.3 1.9 %copy-start.1 = (f32[32,104]{1,0:T(8,128)S(1)}, f32[32,104]{1,0:T(8,128)}, u32[]{:S(2)}) copy-start(f32[32,104]{1,0:T(8,128)} %get-tuple-element.7) | copy-start | bytes 39940
  76.3 2.5 %copy-start = (bf16[3,8,2048]{2,1,0:T(8,128)(2,1)S(1)}, bf16[3,8,2048]{2,1,0:T(8,128)(2,1)}, u32[]{:S(2)}) copy-start(bf16[3,8,2048]{2,1,0:T(8,128)(2,1)} %get-tuple-element.8) | copy-start | bytes 294916

commit v2 on v1

v2 whole, which is shorter than its diff:
```python
import functools

import jax
import jax.numpy as jnp
from jax import lax
from jax.experimental import pallas as pl
from jax.experimental.pallas import tpu as pltpu
from jax.sharding import PartitionSpec as P

MESH = pl.DeviceIdType.MESH
F32 = jnp.float32
BF16 = jnp.bfloat16
OFFSETS = [(i, j) for i in range(3) for j in range(3)]
NEIGHBOURS = [(1, 1), (1, -1), (-1, 1), (-1, -1), (1, 0), (-1, 0), (0, 1), (0, -1)]


def nt(a, b):
    return lax.dot_general(a, b, (((1,), (1,)), ((), ())), preferred_element_type=F32)


def nn(a, b):
    return lax.dot_general(a, b, (((1,), (0,)), ((), ())), preferred_element_type=F32)


def slope(pre):
    s = 1.0 / (1.0 + jnp.exp(-pre))
    return s * (1.0 + pre * (1.0 - s))


def kernel(
    sizes,
    x_any, lab_any, w_any, head_any, match_any,
    cg_any, hg_any, ig_any,
    x_ref, lab_ref, w_ref, head_ref, match_ref, cg_ref, hg_ref, ig_ref,
    xh, gh, xo, go, wt, wpad, tmp, slo, slw, hcat, tcat, hd, hzin, hzout, hall, zin, zout, part,
    pk, rsin, dep, fin,
    in_s, out_s, halo_s, halo_r, hx_s, hx_r, ax_s, ax_r, z_s, z_r, rs_s, rs_r, dp_s, dp_r, ag_s, ag_r,
):
    nx, nd, nr, slab, rows, classes, layers = sizes
    cells = slab * rows * 16
    plane = rows * 16
    own_p, own_r = slice(2, slab + 2), slice(2, rows + 2)
    peer = lax.axis_index("peer")
    depth = lax.axis_index("depth")
    row = lax.axis_index("row")
    xpos, zhalf = lax.div(peer, 2), lax.rem(peer, 2)
    zpos = zhalf * nd + depth

    def near(dp, dr):
        where = {}
        if dr:
            where["row"] = lax.rem(row + dr + nr, nr)
        if dp:
            z = lax.rem(zpos + dp + 2 * nd, 2 * nd)
            where["peer"] = 2 * xpos + lax.div(z, nd)
            where["depth"] = lax.rem(z, nd)
        return where

    def x_mate(s):
        return {"peer": 2 * lax.rem(xpos + s, nx) + zhalf}

    z_mate = {"peer": 2 * xpos + (1 - zhalf)}

    def row_mate(s):
        return {"row": lax.rem(row + s, nr)}

    def depth_mate(s):
        return {"depth": lax.rem(depth + s, nd)}

    loads = [
        pltpu.make_async_copy(src, dst, in_s.at[n])
        for n, (src, dst) in enumerate(
            [(x_any, x_ref), (head_any, head_ref), (w_any, w_ref), (lab_any, lab_ref), (match_any, match_ref)]
        )
    ]
    for load in loads:
        load.start()

    mates = [near(*step) for step in NEIGHBOURS] + [near(2, 0), near(-2, 0)]
    mates += [x_mate(s) for s in range(1, nx)]
    mates += [row_mate(s) for s in range(2, nr - 1)]
    barrier = pltpu.get_barrier_semaphore()
    for mate in mates:
        pl.semaphore_signal(barrier, inc=1, device_id=mate, device_id_type=MESH)

    started = []

    def remote(src, dst, send, recv, mate):
        return pltpu.make_async_remote_copy(
            src_ref=src, dst_ref=dst, send_sem=send, recv_sem=recv, device_id=mate, device_id_type=MESH
        )

    def start(copies):
        for copy in copies:
            copy.start()
        started.extend(copies)
        return copies

    def arrive(copies):
        for copy in copies:
            copy.wait_recv()

    loads[0].wait()
    for d in range(slab):
        for b in range(16):
            tmp[pl.ds(d * plane + b, rows, stride=16), :] = x_ref[d, :, b * 128 : (b + 1) * 128].astype(F32)
    xh[0, own_p, own_r] = tmp[...].reshape(slab, rows, 16, 128).astype(BF16)

    loads[1].wait()
    tmp[0:32, :] = jnp.zeros((32, 128), F32)
    tmp[0:32, 0:classes] = head_ref[...].astype(F32)
    head = tmp[0:32, :].astype(BF16)
    hd[xpos] = head

    pl.semaphore_wait(barrier, len(mates))

    def halo_copies(buf, at, ex):
        copies = []
        for n, (dp, dr) in enumerate(NEIGHBOURS):
            if dp == 0:
                src_p, dst_p = pl.ds(2, slab), pl.ds(2, slab)
            elif dp == 1:
                src_p = pl.ds(slab, 2)
                dst_p = pl.ds(jnp.where(depth == nd - 1, slab + 4, 0), 2)
            else:
                src_p = pl.ds(2, 2)
                dst_p = pl.ds(jnp.where(depth == 0, slab + 6, slab + 2), 2)
            if dr == 0:
                src_r, dst_r = pl.ds(2, rows), pl.ds(2, rows)
            elif dr == 1:
                src_r = pl.ds(rows, 2)
                dst_r = pl.ds(jnp.where(row == nr - 1, rows + 4, 0), 2)
            else:
                src_r = pl.ds(2, 2)
                dst_r = pl.ds(jnp.where(row == 0, rows + 6, rows + 2), 2)
            copies.append(
                remote(
                    buf.at[at, src_p, src_r], buf.at[at, dst_p, dst_r],
                    halo_s.at[ex, n], halo_r.at[ex, n], near(dp, dr),
                )
            )
        return copies

    halo = start(halo_copies(xh, 0, 0))
    head_x = start(
        [remote(hd.at[xpos], hd.at[xpos], hx_s.at[s], hx_r.at[s], x_mate(s)) for s in range(1, nx)]
    )

    def clear_wide(buf, at):
        zero_p = jnp.zeros((2, rows + 4, 16, 128), BF16)
        buf[at, pl.ds(jnp.where(depth == 0, 0, slab + 4), 2), 0 : rows + 4] = zero_p
        buf[at, pl.ds(jnp.where(depth == nd - 1, slab + 2, slab + 6), 2), 0 : rows + 4] = zero_p
        zero_r = jnp.zeros((slab + 4, 2, 16, 128), BF16)
        buf[at, 0 : slab + 4, pl.ds(jnp.where(row == 0, 0, rows + 4), 2)] = zero_r
        buf[at, 0 : slab + 4, pl.ds(jnp.where(row == nr - 1, rows + 2, rows + 6), 2)] = zero_r

    def put_near(buf, at, value):
        buf[at, 0 : slab + 2, 0 : rows + 2] = value.astype(BF16)
        zero_p = jnp.zeros((1, rows + 2, 16, 128), BF16)
        buf[at, pl.ds(jnp.where(depth == 0, 0, slab + 2), 1), 0 : rows + 2] = zero_p
        buf[at, pl.ds(jnp.where(depth == nd - 1, slab + 1, slab + 3), 1), 0 : rows + 2] = zero_p
        zero_r = jnp.zeros((slab + 2, 1, 16, 128), BF16)
        buf[at, 0 : slab + 2, pl.ds(jnp.where(row == 0, 0, rows + 2), 1)] = zero_r
        buf[at, 0 : slab + 2, pl.ds(jnp.where(row == nr - 1, rows + 1, rows + 3), 1)] = zero_r

    for at in range(2):
        clear_wide(xh, at)
        clear_wide(gh, at)
    hcat[...] = jnp.zeros_like(hcat)
    tcat[...] = jnp.zeros_like(tcat)
    for a in range(4):
        hcat[a * 32 : (a + 1) * 32, a * 128 : (a + 1) * 128] = head

    lane = lax.broadcasted_iota(jnp.int32, (1, 16, 128), 2)
    block = lax.broadcasted_iota(jnp.int32, (1, 16, 128), 1)
    low = lane < 64
    inside = jnp.where(low, block, 15 - block) > 0

    def spill(y, shape):
        e = y[:, 128:].reshape(-1, 16, 128)
        moved = jnp.where(low, pltpu.roll(e, 1, 1), pltpu.roll(e, 15, 1))
        return (y[:, :128].reshape(-1, 16, 128) + jnp.where(inside, moved, 0.0)).reshape(*shape, 16, 128)

    loads[2].wait()
    wpad[:, 0 : 27 * 32] = w_ref[...].reshape(layers * 32, 27 * 32).astype(F32)
    wt[:, 1, 1:3] = jnp.zeros((9, 2, layers * 32, 128), BF16)
    group = lax.div(lax.broadcasted_iota(jnp.int32, (layers * 32, 128), 1), 32)

    def rolled(v, groups):
        shift = (groups * 32) % 128
        return v if shift == 0 else pltpu.roll(v, shift, 1)

    for ij in range(9):
        blk = None
        for k in range(3):
            t, g = divmod(3 * ij + k, 4)
            piece = rolled(wpad[:, t * 128 : (t + 1) * 128], k - g)
            blk = piece if blk is None else jnp.where(group == k, piece, blk)
        r0 = rolled(blk, -1)
        wt[ij, 0, 0] = jnp.where(group < 2, r0, 0.0).astype(BF16)
        wt[ij, 1, 0] = jnp.where(group == 3, r0, 0.0).astype(BF16)
        wt[ij, 0, 1] = jnp.where(group < 3, blk, 0.0).astype(BF16)
        wt[ij, 0, 2] = jnp.where(group > 0, rolled(blk, 1), 0.0).astype(BF16)
        r3 = rolled(blk, 2)
        wt[ij, 0, 3] = jnp.where(group > 1, r3, 0.0).astype(BF16)
        wt[ij, 1, 3] = jnp.where(group == 0, r3, 0.0).astype(BF16)

    def weights(layer, ij, half):
        return wt[ij, half, :, layer * 32 : (layer + 1) * 32, :].reshape(128, 128)

    def windows(buf, at, shape, base, order):
        return jnp.concatenate(
            [
                buf[at, base + i : base + i + shape[0], base + j : base + j + shape[1]].reshape(-1, 128)
                for i, j in order
            ],
            axis=1,
        )

    def forward(layer, cols, shape):
        band = jnp.concatenate(
            [jnp.concatenate([weights(layer, ij, 0), weights(layer, ij, 1)], axis=0) for ij in range(9)], axis=1
        )
        return spill(nt(cols, band), shape)

    def backward(layer, cols, shape):
        band = jnp.concatenate(
            [jnp.concatenate([weights(layer, ij, 0), weights(layer, ij, 1)], axis=1) for ij in range(9)], axis=0
        )
        return spill(nn(cols, band), shape)

    def silu(y):
        return (y / (1.0 + jnp.exp(-y))).astype(BF16)

    def slope_of(y):
        return slope(y.astype(BF16).astype(F32))

    mine = (slab, rows)
    wide = (slab + 2, rows + 2)
    mirrored = [(2 - i, 2 - j) for i, j in OFFSETS]

    loads[3].wait()
    loads[4].wait()

    for pair in range(2):
        arrive(halo)
        y = forward(2 * pair, windows(xh, pair, wide, 0, OFFSETS), wide)
        put_near(xo, pair, silu(y))
        y2 = forward(2 * pair + 1, windows(xo, pair, mine, 0, OFFSETS), mine)
        act = silu(y2)
        if pair == 0:
            xh[1, own_p, own_r] = act
            halo = start(halo_copies(xh, 1, 1))
        else:
            for d in range(slab):
                hall[d][xpos] = act[d].reshape(plane, 128)
            act_x = [
                start(
                    [
                        remote(hall[d].at[xpos], hall[d].at[xpos], ax_s.at[d, s], ax_r.at[d, s], x_mate(s))
                        for s in X_ORDER(nx)
                    ]
                )
                for d in range(slab)
            ]
            arrive(head_x)
            for d in range(slab):
                hzout[d] = hd[lax.div(match_ref[d, 2 * xpos + (1 - zhalf)], 2)]
            head_z = start([remote(hzout, hzin, z_s.at[slab], z_r.at[slab], z_mate)])
        slw[pair] = slope_of(y)
        slo[pair] = slope_of(y2)

    hidden = act.reshape(cells, 128)

    col_class = lax.broadcasted_iota(jnp.int32, (plane, 128), 1)
    real = col_class < classes
    spread_r = lax.broadcasted_iota(jnp.int32, (cells, slab * rows), 0)
    spread_c = lax.broadcasted_iota(jnp.int32, (cells, slab * rows), 1)
    spread = jnp.where(lax.div(spread_r, 16) == spread_c, 1.0, 0.0).astype(BF16)
    lab = nn(spread, lab_ref[...].reshape(slab * rows, 64).astype(F32).astype(BF16))
    vox = lax.broadcasted_iota(jnp.int32, (cells, 64), 1)
    own = lax.rem(lax.broadcasted_iota(jnp.int32, (cells, 64), 0), 16)
    lab = jnp.where(lax.div(vox, 4) == own, lab, 0.0).astype(BF16)
    pick_r = lax.broadcasted_iota(jnp.int32, (64, 512), 0)
    pick_c = lax.broadcasted_iota(jnp.int32, (64, 512), 1)
    pick = jnp.where(lax.rem(pick_r, 4) == lax.div(pick_c, 128), 1.0, 0.0).astype(BF16)
    class_of = nn(lab, pick)

    def softmax(act_plane, heads):
        logits = nn(act_plane, heads)
        out = []
        for a in range(4):
            ex = jnp.where(real, jnp.exp(logits[:, a * 128 : (a + 1) * 128]), 0.0)
            out.append(ex / jnp.sum(ex, axis=1, keepdims=True))
        return out

    col_f = col_class.astype(F32)
    for d in range(slab):
        probs = softmax(hidden[d * plane : (d + 1) * plane], hcat[...])
        for a in range(4):
            mark = jnp.where(class_of[d * plane : (d + 1) * plane, a * 128 : (a + 1) * 128] == col_f, 0.5, 0.0)
            part[d, :, a * 128 : (a + 1) * 128] = probs[a] - mark

    act_z = []
    for d in range(slab):
        arrive(act_x[d])
        zout[d] = hall[d][lax.div(match_ref[d, 2 * xpos + (1 - zhalf)], 2)]
        act_z.append(start([remote(zout.at[d], zin.at[d], z_s.at[d], z_r.at[d], z_mate)]))
    arrive(head_z)
    grad_rows = []
    for d in range(slab):
        source = match_ref[d, peer]
        near_half = lax.rem(source, 2) == zhalf
        near_at = lax.div(source, 2)
        target_head = jnp.where(near_half, hd[near_at].astype(F32), hzin[d].astype(F32)).astype(BF16)
        for a in range(4):
            tcat[d, a * 32 : (a + 1) * 32, a * 128 : (a + 1) * 128] = target_head
        arrive(act_z[d])
        target_act = jnp.where(near_half, hall[d][near_at].astype(F32), zin[d].astype(F32)).astype(BF16)
        target = softmax(target_act, tcat[d])
        grad_rows.append(
            jnp.concatenate(
                [
                    (part[d, :, a * 128 : (a + 1) * 128] - 0.5 * target[a].astype(BF16).astype(F32)).astype(BF16)
                    for a in range(4)
                ],
                axis=1,
            )
        )
    dlogits = jnp.concatenate(grad_rows, axis=0)
    g = nt(dlogits, hcat[...]).reshape(slab, rows, 16, 128) * slo[1]

    group32 = lax.div(lax.broadcasted_iota(jnp.int32, (32, 128), 1), 32)
    group288 = lax.div(lax.broadcasted_iota(jnp.int32, (288, 128), 1), 32)
    own_chunks = 8 // nr
    from_next = lane < 32
    from_last = lane >= 96

    def weight_grad(layer, g, cols):
        g = g.reshape(-1, 16, 128)
        ahead = jnp.where(from_next & (block < 15), pltpu.roll(g, 15, 1), 0.0)
        edge = jnp.where(from_last & (block > 0), pltpu.roll(g, 1, 1), ahead)
        both = jnp.concatenate([g.reshape(cells, 128), edge.reshape(cells, 128)], axis=1).astype(BF16).T
        prod = nn(both, cols)

        def take(at):
            return jnp.concatenate([prod[at : at + 32, ij * 128 : (ij + 1) * 128] for ij in range(9)], axis=0)

        s0 = jnp.where(group288 == 3, take(128), take(0))
        s3 = jnp.where(group288 == 0, take(224), take(96))
        total = take(32) + pltpu.roll(s0, 32, 1) + pltpu.roll(take(64), 96, 1) + pltpu.roll(s3, 64, 1)
        for t in range(7):
            tile = None
            ks = [(gr, *divmod(4 * t + gr, 3)) for gr in range(4) if 4 * t + gr < 27]
            for ij in sorted({ij for _, ij, _ in ks}):
                first = [(gr, k) for gr, at, k in ks if at == ij][0]
                moved = rolled(total[ij * 32 : (ij + 1) * 32], first[0] - first[1])
                tile = moved if tile is None else jnp.where(group32 >= first[0], moved, tile)
            pk[layer, t // own_chunks, t % own_chunks] = tile.astype(BF16)
        if layer < layers - 1:
            pk[layer, 7 // own_chunks, 7 % own_chunks] = jnp.zeros((32, 128), BF16)

    def span(layer_set):
        return pl.ds(layer_set[0], len(layer_set)), layer_set[0]

    def send_row(layer_set):
        at, n = span(layer_set)
        return start(
            [
                remote(pk.at[at, lax.rem(row + s, nr)], rsin.at[at, s], rs_s.at[n, s], rs_r.at[n, s], row_mate(s))
                for s in range(1, nr)
            ]
        )

    def send_depth(layer_set, copies):
        arrive(copies)
        at, n = span(layer_set)
        for layer in layer_set:
            total = pk[layer, row].astype(F32)
            for s in range(1, nr):
                total = total + rsin[layer, s].astype(F32)
            dep[layer, depth] = total.astype(BF16)
        return start(
            [
                remote(dep.at[at, depth], dep.at[at, depth], dp_s.at[n, s], dp_r.at[n, s], depth_mate(s))
                for s in range(1, nd)
            ]
        )

    def send_all(layer_set, copies):
        arrive(copies)
        at, n = span(layer_set)
        for layer in layer_set:
            total = dep[layer, 0].astype(F32)
            for s in range(1, nd):
                total = total + dep[layer, s].astype(F32)
            fin[layer, row] = total.astype(BF16)
        return start(
            [
                remote(fin.at[at, row], fin.at[at, row], ag_s.at[n, s], ag_r.at[n, s], row_mate(s))
                for s in range(1, nr)
            ]
        )

    stores = []

    def store(src, dst):
        copy = pltpu.make_async_copy(src, dst, out_s.at[len(stores)])
        copy.start()
        stores.append(copy)

    def finish(layer_set, copies):
        arrive(copies)
        at, _ = span(layer_set)
        for layer in layer_set:
            for t in range(7):
                lanes = min(128, 27 * 32 - t * 128)
                cg_ref[layer, :, t * 128 : t * 128 + lanes] = fin[layer, t // own_chunks, t % own_chunks].astype(F32)[:, :lanes]
            if layer == layers - 1:
                hg_ref[...] = fin[layer, 7 // own_chunks, 7 % own_chunks].astype(F32)[:, :classes]
                store(hg_ref, hg_any)
        store(cg_ref.at[at], cg_any.at[at])

    gh[1, own_p, own_r] = g.astype(BF16)
    halo = start(halo_copies(gh, 1, 3))
    wide_heads = nn(hidden.T, dlogits)
    heads = wide_heads[0:32, 0:128]
    for a in range(1, 4):
        heads = heads + wide_heads[a * 32 : (a + 1) * 32, a * 128 : (a + 1) * 128]
    pk[3, 7 // own_chunks, 7 % own_chunks] = heads.astype(BF16)
    weight_grad(3, g, windows(xo, 1, mine, 0, OFFSETS))
    first = send_row([3])
    arrive(halo)
    g3 = backward(3, windows(gh, 1, wide, 0, mirrored), wide) * slw[1]
    put_near(go, 1, g3)
    g2 = backward(2, windows(go, 1, mine, 0, mirrored), mine) * slo[0]
    gh[0, own_p, own_r] = g2.astype(BF16)
    halo = start(halo_copies(gh, 0, 2))
    weight_grad(2, g3[1 : slab + 1, 1 : rows + 1], windows(xh, 1, mine, 1, OFFSETS))
    weight_grad(1, g2, windows(xo, 0, mine, 0, OFFSETS))
    second = send_row([1, 2])
    first = send_depth([3], first)
    arrive(halo)
    g1 = backward(1, windows(gh, 0, wide, 0, mirrored), wide) * slw[0]
    put_near(go, 0, g1)
    weight_grad(0, g1[1 : slab + 1, 1 : rows + 1], windows(xh, 0, mine, 1, OFFSETS))
    last = send_row([0])
    second = send_depth([1, 2], second)
    first = send_all([3], first)
    back = backward(0, windows(go, 0, mine, 0, mirrored), mine)
    tmp[...] = back.reshape(cells, 128)
    for d in range(slab):
        for b in range(16):
            ig_ref[d, :, b * 128 : (b + 1) * 128] = tmp[pl.ds(d * plane + b, rows, stride=16), :].astype(BF16)
    store(ig_ref, ig_any)
    last = send_depth([0], last)
    second = send_all([1, 2], second)
    finish([3], first)
    last = send_all([0], last)
    finish([1, 2], second)
    for copy in started:
        copy.wait_send()
    finish([0], last)
    for copy in stores:
        copy.wait()


def X_ORDER(nx):
    return [s for s in (2, 1, 3) if s < nx]


def solution(mesh):
    np_, nd, nr = mesh.shape["peer"], mesh.shape["depth"], mesh.shape["row"]
    nx = np_ // 2

    def body(features, labels, conv_weights, head_weights, matching):
        slab, rows, merged = features.shape
        layers = conv_weights.shape[1]
        classes = head_weights.shape[2]
        cells = slab * rows * 16
        chunk = (8 // nr, 32, 128)
        far = (2, slab + 8, rows + 8, 16, 128)
        close = (2, slab + 4, rows + 4, 16, 128)
        anywhere = pl.BlockSpec(memory_space=pl.ANY)
        dma = pltpu.SemaphoreType.DMA
        scratch = [
            pltpu.VMEM((slab, rows, merged), BF16),
            pltpu.VMEM((slab, rows, merged // 32), jnp.int32),
            pltpu.VMEM((layers, 32, 27 * 32), BF16),
            pltpu.VMEM((32, classes), BF16),
            pltpu.SMEM((slab, np_), jnp.int32),
            pltpu.VMEM((layers, 32, 27 * 32), F32),
            pltpu.VMEM((32, classes), F32),
            pltpu.VMEM((slab, rows, merged), BF16),
            pltpu.VMEM(far, BF16),
            pltpu.VMEM(far, BF16),
            pltpu.VMEM(close, BF16),
            pltpu.VMEM(close, BF16),
            pltpu.VMEM((9, 2, 4, layers * 32, 128), BF16),
            pltpu.VMEM((layers * 32, 896), F32),
            pltpu.VMEM((cells, 128), F32),
            pltpu.VMEM((2, slab, rows, 16, 128), F32),
            pltpu.VMEM((2, slab + 2, rows + 2, 16, 128), F32),
            pltpu.VMEM((128, 512), BF16),
            pltpu.VMEM((slab, 128, 512), BF16),
            pltpu.VMEM((nx, 32, 128), BF16),
            pltpu.VMEM((slab, 32, 128), BF16),
            pltpu.VMEM((slab, 32, 128), BF16),
            [pltpu.VMEM((nx, rows * 16, 128), BF16) for _ in range(slab)],
            pltpu.VMEM((slab, rows * 16, 128), BF16),
            pltpu.VMEM((slab, rows * 16, 128), BF16),
            pltpu.VMEM((slab, rows * 16, 512), F32),
            pltpu.VMEM((layers, nr) + chunk, BF16),
            pltpu.VMEM((layers, nr) + chunk, BF16),
            pltpu.VMEM((layers, nd) + chunk, BF16),
            pltpu.VMEM((layers, nr) + chunk, BF16),
            dma((5,)), dma((5,)),
            dma((4, 8)), dma((4, 8)),
            dma((nx,)), dma((nx,)),
            dma((slab, nx)), dma((slab, nx)),
            dma((slab + 1,)), dma((slab + 1,)),
            dma((layers, nr)), dma((layers, nr)),
            dma((layers, nd)), dma((layers, nd)),
            dma((layers, nr)), dma((layers, nr)),
        ]
        sizes = (nx, nd, nr, slab, rows, classes, layers)
        cg, hg, ig = pl.pallas_call(
            functools.partial(kernel, sizes),
            out_shape=(
                jax.ShapeDtypeStruct((layers, 32, 27 * 32), F32),
                jax.ShapeDtypeStruct((32, classes), F32),
                jax.ShapeDtypeStruct((slab, rows, merged), BF16),
            ),
            in_specs=[anywhere] * 5,
            out_specs=(anywhere,) * 3,
            scratch_shapes=scratch,
            compiler_params=pltpu.CompilerParams(collective_id=0, has_side_effects=True),
        )(
            features,
            labels,
            conv_weights[0].transpose(0, 2, 1),
            head_weights[0],
            matching,
        )
        return cg.transpose(0, 2, 1)[None], hg[None], ig[None]

    return jax.shard_map(
        body,
        mesh=mesh,
        in_specs=(
            P("depth", "row", None),
            P("depth", "row", None),
            P("peer", None, None, None),
            P("peer", None, None),
            P("depth", None),
        ),
        out_specs=(
            P("peer", None, None, None),
            P("peer", None, None),
            P("peer", "depth", "row", None),
        ),
        check_vma=False,
    )
```

time: 79.6 us -> 64.6 us (0.81)
  Pallas kernels: 75.7 us -> 60.8 us
    pallas_call x1, Pallas kernels: 75.7 us -> 60.8 us  [body(): pl.pallas_call(functools.partial(kernel, sizes), out_shape=(jax.ShapeDtyp...]
where the time goes in v2:
time: 64.6 us; the launch traced here: 64.5 us
  Pallas kernels  60.8 us (94%)
  local copies, waits for them, and re-layouts  3.1 us (5%)
  between operations  0.66 us (1%)
    pallas_call x1, Pallas kernels, body(): pl.pallas_call(functools.partial(kernel, sizes), out_shape=(jax.ShapeDtyp...  60.8 us
    unnamed x7, local copies, waits for them, and re-layouts  3.1 us

profile of v2, /device:TPU:1, one launch (start us, length us, event | category | flops | bytes accessed | tf_op | source)
XLA Modules:
  0.0 64.5 jit_solution(15390852327704646241)
XLA Ops:
  0.6 60.8 %shard_map.76 = (f32[4,32,864]{2,1,0:T(8,128)}, f32[32,104]{1,0:T(8,128)}, bf16[3,8,2048]{2,1,0:T(8,128)(2,1)}) custom-call(bf16[3,8,2048]{2,1,0:T(8,128)(2,1)} %x_any.1, s32[3,8,64]{2,1,0:T(8,128)} %lab_any.1, bf16[4,32,864]{2,1,0:T(8,128)(2,1)} %bitcast.10, bf16[32,104]{1,0:T(8,128)(2,1)} %bitcast.13, s32[3,8]{1,0:T(4,128)} %match_any.1), custom_call_target="tpu_custom_call" | custom-call | tf_op jit(solution)/shard_map/pallas_call | solution.py:527
  61.4 0.0 copy-start.1
  61.4 0.0 copy-start
  61.4 1.9 %copy.11 = f32[1,4,864,32]{2,3,1,0:T(8,128)} copy(f32[1,4,864,32]{2,3,1,0:T(8,128)} %bitcast.9) | data formatting | bytes 884736
  63.3 0.0 copy-done.1
  63.3 0.6 copy.12
  63.9 0.0 copy-done
  63.9 0.6 copy.13
Async XLA Ops:
  61.4 1.9 %copy-start.1 = (f32[32,104]{1,0:T(8,128)S(1)}, f32[32,104]{1,0:T(8,128)}, u32[]{:S(2)}) copy-start(f32[32,104]{1,0:T(8,128)} %get-tuple-element.7) | copy-start | bytes 39940
  61.4 2.5 %copy-start = (bf16[3,8,2048]{2,1,0:T(8,128)(2,1)S(1)}, bf16[3,8,2048]{2,1,0:T(8,128)(2,1)}, u32[]{:S(2)}) copy-start(bf16[3,8,2048]{2,1,0:T(8,128)(2,1)} %get-tuple-element.8) | copy-start | bytes 294916

commit v3 on v2

--- a/solution.py
+++ b/solution.py
@@ -30,11 +30,11 @@
 def kernel(
     sizes,
     x_any, lab_any, w_any, head_any, match_any,
-    cg_any, hg_any, ig_any,
-    x_ref, lab_ref, w_ref, head_ref, match_ref, cg_ref, hg_ref, ig_ref,
+    cg_ref, hg_ref, ig_ref,
+    x_ref, lab_ref, w_ref, head_ref, match_ref,
     xh, gh, xo, go, wt, wpad, tmp, slo, slw, hcat, tcat, hd, hzin, hzout, hall, zin, zout, part,
     pk, rsin, dep, fin,
-    in_s, out_s, halo_s, halo_r, hx_s, hx_r, ax_s, ax_r, z_s, z_r, rs_s, rs_r, dp_s, dp_r, ag_s, ag_r,
+    in_s, halo_s, halo_r, hx_s, hx_r, ax_s, ax_r, z_s, z_r, rs_s, rs_r, dp_s, dp_r, ag_s, ag_r,
 ):
     nx, nd, nr, slab, rows, classes, layers = sizes
     cells = slab * rows * 16
@@ -402,24 +402,14 @@
             ]
         )
 
-    stores = []
-
-    def store(src, dst):
-        copy = pltpu.make_async_copy(src, dst, out_s.at[len(stores)])
-        copy.start()
-        stores.append(copy)
-
     def finish(layer_set, copies):
         arrive(copies)
-        at, _ = span(layer_set)
         for layer in layer_set:
             for t in range(7):
                 lanes = min(128, 27 * 32 - t * 128)
                 cg_ref[layer, :, t * 128 : t * 128 + lanes] = fin[layer, t // own_chunks, t % own_chunks].astype(F32)[:, :lanes]
             if layer == layers - 1:
                 hg_ref[...] = fin[layer, 7 // own_chunks, 7 % own_chunks].astype(F32)[:, :classes]
-                store(hg_ref, hg_any)
-        store(cg_ref.at[at], cg_any.at[at])
 
     gh[1, own_p, own_r] = g.astype(BF16)
     halo = start(halo_copies(gh, 1, 3))
@@ -452,7 +442,6 @@
     for d in range(slab):
         for b in range(16):
             ig_ref[d, :, b * 128 : (b + 1) * 128] = tmp[pl.ds(d * plane + b, rows, stride=16), :].astype(BF16)
-    store(ig_ref, ig_any)
     last = send_depth([0], last)
     second = send_all([1, 2], second)
     finish([3], first)
@@ -461,7 +450,16 @@
     for copy in started:
         copy.wait_send()
     finish([0], last)
-    for copy in stores:
+
+
+def write_out(cg_ref, hg_ref, ig_ref, cg_out, hg_out, ig_out, sem):
+    copies = [
+        pltpu.make_async_copy(src, dst, sem.at[n])
+        for n, (src, dst) in enumerate([(cg_ref, cg_out), (ig_ref, ig_out), (hg_ref, hg_out)])
+    ]
+    for copy in copies:
+        copy.start()
+    for copy in copies:
         copy.wait()
 
 
@@ -481,7 +479,8 @@
         chunk = (8 // nr, 32, 128)
         far = (2, slab + 8, rows + 8, 16, 128)
         close = (2, slab + 4, rows + 4, 16, 128)
-        anywhere = pl.BlockSpec(memory_space=pl.ANY)
+        vmem = pl.BlockSpec(memory_space=pltpu.VMEM)
+        hbm = pl.BlockSpec(memory_space=pltpu.HBM)
         dma = pltpu.SemaphoreType.DMA
         scratch = [
             pltpu.VMEM((slab, rows, merged), BF16),
@@ -489,9 +488,6 @@
             pltpu.VMEM((layers, 32, 27 * 32), BF16),
             pltpu.VMEM((32, classes), BF16),
             pltpu.SMEM((slab, np_), jnp.int32),
-            pltpu.VMEM((layers, 32, 27 * 32), F32),
-            pltpu.VMEM((32, classes), F32),
-            pltpu.VMEM((slab, rows, merged), BF16),
             pltpu.VMEM(far, BF16),
             pltpu.VMEM(far, BF16),
             pltpu.VMEM(close, BF16),
@@ -514,7 +510,7 @@
             pltpu.VMEM((layers, nr) + chunk, BF16),
             pltpu.VMEM((layers, nd) + chunk, BF16),
             pltpu.VMEM((layers, nr) + chunk, BF16),
-            dma((5,)), dma((5,)),
+            dma((5,)),
             dma((4, 8)), dma((4, 8)),
             dma((nx,)), dma((nx,)),
             dma((slab, nx)), dma((slab, nx)),
@@ -527,21 +523,28 @@
         cg, hg, ig = pl.pallas_call(
             functools.partial(kernel, sizes),
             out_shape=(
-                jax.ShapeDtypeStruct((layers, 32, 27 * 32), F32),
-                jax.ShapeDtypeStruct((32, classes), F32),
-                jax.ShapeDtypeStruct((slab, rows, merged), BF16),
+                pltpu.VMEM((layers, 32, 27 * 32), F32),
+                pltpu.VMEM((32, classes), F32),
+                pltpu.VMEM((slab, rows, merged), BF16),
             ),
-            in_specs=[anywhere] * 5,
-            out_specs=(anywhere,) * 3,
+            in_specs=[hbm] * 5,
+            out_specs=(vmem,) * 3,
             scratch_shapes=scratch,
-            compiler_params=pltpu.CompilerParams(collective_id=0, has_side_effects=True),
+            compiler_params=pltpu.CompilerParams(collective_id=0, has_side_effects=True, vmem_limit_bytes=40 * 2**20),
         )(
-            features,
-            labels,
-            conv_weights[0].transpose(0, 2, 1),
-            head_weights[0],
-            matching,
-        )
+            *(
+                pltpu.with_memory_space_constraint(v, pltpu.HBM)
+                for v in (features, labels, conv_weights[0].transpose(0, 2, 1), head_weights[0], matching)
+            )
+        )
+        cg, hg, ig = pl.pallas_call(
+            write_out,
+            out_shape=tuple(jax.ShapeDtypeStruct(v.shape, v.dtype) for v in (cg, hg, ig)),
+            in_specs=[vmem] * 3,
+            out_specs=(hbm,) * 3,
+            scratch_shapes=[dma((3,))],
+            compiler_params=pltpu.CompilerParams(vmem_limit_bytes=2**20),
+        )(cg, hg, ig)
         return cg.transpose(0, 2, 1)[None], hg[None], ig[None]
 
     return jax.shard_map(

time: 64.6 us -> 61.6 us (0.954)
  local copies, waits for them, and re-layouts: 3.1 us -> 0 us
    unnamed x7 -> x0, local copies, waits for them, and re-layouts: 3.1 us -> none
    pallas_call x1 -> x2, Pallas kernels: 60.8 us -> 60.9 us  [the longest x1 60.1 us: body(): pl.pallas_call(functools.partial(kernel, sizes), out_shape=(pltpu.VMEM((l...]
where the time goes in v3:
time: 61.6 us; the launch traced here: 61.5 us
  Pallas kernels  60.9 us (99%)
  between operations  0.64 us (1%)
    pallas_call x1, Pallas kernels, body(): pl.pallas_call(functools.partial(kernel, sizes), out_shape=(pltpu.VMEM((l...  60.1 us

profile of v3, /device:TPU:1, one launch (start us, length us, event | category | flops | bytes accessed | tf_op | source)
XLA Modules:
  0.0 61.5 jit_solution(2419772741590054640)
XLA Ops:
  0.6 60.1 %shard_map.76 = (f32[4,32,864]{2,1,0:T(8,128)S(1)}, f32[32,104]{1,0:T(8,128)S(1)}, bf16[3,8,2048]{2,1,0:T(8,128)(2,1)S(1)}) custom-call(bf16[3,8,2048]{2,1,0:T(8,128)(2,1)} %x_any.1, s32[3,8,64]{2,1,0:T(8,128)} %lab_any.1, bf16[4,32,864]{2,1,0:T(8,128)(2,1)} %bitcast.9, bf16[32,104]{1,0:T(8,128)(2,1)} %bitcast.10, s32[3,8]{1,0:T(4,128)} %match_any.1), custom_call_target="tpu_custom_call" | custom-call | tf_op jit(solution)/shard_map/pallas_call | solution.py:523
  60.7 0.8 %shard_map.77 = (f32[4,32,864]{2,1,0:T(8,128)}, f32[32,104]{1,0:T(8,128)}, bf16[3,8,2048]{2,1,0:T(8,128)(2,1)}) custom-call(f32[4,32,864]{2,1,0:T(8,128)S(1)} %get-tuple-element.9.cg_ref, f32[32,104]{1,0:T(8,128)S(1)} %get-tuple-element.10.hg_ref, bf16[3,8,2048]{2,1,0:T(8,128)(2,1)S(1)} %get-tuple-element.11.ig_ref), custom_call_target="tpu_custom_call" | custom-call | tf_op jit(solution)/shard_map/pallas_call | solution.py:540

commit v4 on v3

--- a/solution.py
+++ b/solution.py
@@ -32,13 +32,14 @@
     x_any, lab_any, w_any, head_any, match_any,
     cg_ref, hg_ref, ig_ref,
     x_ref, lab_ref, w_ref, head_ref, match_ref,
-    xh, gh, xo, go, wt, wpad, tmp, slo, slw, hcat, tcat, hd, hzin, hzout, hall, zin, zout, part,
+    xh, gh, xo, go, wt, wpad, tmp, slo, slw, hcat, tcat, hd, hzin, hzout, hall, zin, zout, far_in, far_out, pick_in, pick_out, part,
     pk, rsin, dep, fin,
-    in_s, halo_s, halo_r, hx_s, hx_r, ax_s, ax_r, z_s, z_r, rs_s, rs_r, dp_s, dp_r, ag_s, ag_r,
+    in_s, halo_s, halo_r, hx_s, hx_r, ax_s, ax_r, z_s, z_r, bx_s, bx_r, bz_s, bz_r, rs_s, rs_r, dp_s, dp_r, ag_s, ag_r,
 ):
     nx, nd, nr, slab, rows, classes, layers = sizes
     cells = slab * rows * 16
     plane = rows * 16
+    part_rows = plane // 2
     own_p, own_r = slice(2, slab + 2), slice(2, rows + 2)
     peer = lax.axis_index("peer")
     depth = lax.axis_index("depth")
@@ -253,7 +254,10 @@
             halo = start(halo_copies(xh, 1, 1))
         else:
             for d in range(slab):
-                hall[d][xpos] = act[d].reshape(plane, 128)
+                tiles = act[d].reshape(plane, 128)
+                hall[d][xpos] = tiles[:part_rows]
+                far_out[d] = tiles[part_rows:]
+            far = [start([remote(far_out.at[d], far_in.at[d], bz_s.at[d], bz_r.at[d], z_mate)]) for d in range(slab)]
             act_x = [
                 start(
                     [
@@ -306,6 +310,26 @@
         arrive(act_x[d])
         zout[d] = hall[d][lax.div(match_ref[d, 2 * xpos + (1 - zhalf)], 2)]
         act_z.append(start([remote(zout.at[d], zin.at[d], z_s.at[d], z_r.at[d], z_mate)]))
+    act_b = []
+    for d in range(slab):
+        arrive(far[d])
+        for s in range(nx):
+            source = match_ref[d, 2 * lax.rem(xpos + s, nx) + zhalf]
+            chosen = jnp.where(
+                lax.rem(source, 2) == zhalf, far_out[d].astype(F32), far_in[d].astype(F32)
+            ).astype(BF16)
+            if s == 0:
+                pick_in[d][xpos] = chosen
+            else:
+                pick_out[s, d] = chosen
+        act_b.append(
+            start(
+                [
+                    remote(pick_out.at[s, d], pick_in[d].at[xpos], bx_s.at[d, s], bx_r.at[d, s], x_mate(s))
+                    for s in X_ORDER(nx)
+                ]
+            )
+        )
     arrive(head_z)
     grad_rows = []
     for d in range(slab):
@@ -316,7 +340,14 @@
         for a in range(4):
             tcat[d, a * 32 : (a + 1) * 32, a * 128 : (a + 1) * 128] = target_head
         arrive(act_z[d])
-        target_act = jnp.where(near_half, hall[d][near_at].astype(F32), zin[d].astype(F32)).astype(BF16)
+        arrive(act_b[d])
+        target_act = jnp.concatenate(
+            [
+                jnp.where(near_half, hall[d][near_at].astype(F32), zin[d].astype(F32)).astype(BF16),
+                pick_in[d][near_at],
+            ],
+            axis=0,
+        )
         target = softmax(target_act, tcat[d])
         grad_rows.append(
             jnp.concatenate(
@@ -433,18 +464,18 @@
     arrive(halo)
     g1 = backward(1, windows(gh, 0, wide, 0, mirrored), wide) * slw[0]
     put_near(go, 0, g1)
+    first = send_all([3], first)
     weight_grad(0, g1[1 : slab + 1, 1 : rows + 1], windows(xh, 0, mine, 1, OFFSETS))
     last = send_row([0])
     second = send_depth([1, 2], second)
-    first = send_all([3], first)
     back = backward(0, windows(go, 0, mine, 0, mirrored), mine)
     tmp[...] = back.reshape(cells, 128)
     for d in range(slab):
         for b in range(16):
             ig_ref[d, :, b * 128 : (b + 1) * 128] = tmp[pl.ds(d * plane + b, rows, stride=16), :].astype(BF16)
-    last = send_depth([0], last)
     second = send_all([1, 2], second)
     finish([3], first)
+    last = send_depth([0], last)
     last = send_all([0], last)
     finish([1, 2], second)
     for copy in started:
@@ -502,9 +533,13 @@
             pltpu.VMEM((nx, 32, 128), BF16),
             pltpu.VMEM((slab, 32, 128), BF16),
             pltpu.VMEM((slab, 32, 128), BF16),
-            [pltpu.VMEM((nx, rows * 16, 128), BF16) for _ in range(slab)],
-            pltpu.VMEM((slab, rows * 16, 128), BF16),
-            pltpu.VMEM((slab, rows * 16, 128), BF16),
+            [pltpu.VMEM((nx, rows * 8, 128), BF16) for _ in range(slab)],
+            pltpu.VMEM((slab, rows * 8, 128), BF16),
+            pltpu.VMEM((slab, rows * 8, 128), BF16),
+            pltpu.VMEM((slab, rows * 8, 128), BF16),
+            pltpu.VMEM((slab, rows * 8, 128), BF16),
+            [pltpu.VMEM((nx, rows * 8, 128), BF16) for _ in range(slab)],
+            pltpu.VMEM((nx, slab, rows * 8, 128), BF16),
             pltpu.VMEM((slab, rows * 16, 512), F32),
             pltpu.VMEM((layers, nr) + chunk, BF16),
             pltpu.VMEM((layers, nr) + chunk, BF16),
@@ -515,6 +550,8 @@
             dma((nx,)), dma((nx,)),
             dma((slab, nx)), dma((slab, nx)),
             dma((slab + 1,)), dma((slab + 1,)),
+            dma((slab, nx)), dma((slab, nx)),
+            dma((slab,)), dma((slab,)),
             dma((layers, nr)), dma((layers, nr)),
             dma((layers, nd)), dma((layers, nd)),
             dma((layers, nr)), dma((layers, nr)),

time: 61.6 us -> 61.6 us (level)
  no operation moved by 1% of the time
where the time goes in v4:
time: 61.6 us; the launch traced here: 61.5 us
  Pallas kernels  60.9 us (99%)
  between operations  0.64 us (1%)
    pallas_call x1, Pallas kernels, body(): pl.pallas_call(functools.partial(kernel, sizes), out_shape=(pltpu.VMEM((l...  60 us

profile of v4, /device:TPU:1, one launch (start us, length us, event | category | flops | bytes accessed | tf_op | source)
XLA Modules:
  0.0 61.5 jit_solution(9103380428916056860)
XLA Ops:
  0.6 60.0 %shard_map.76 = (f32[4,32,864]{2,1,0:T(8,128)S(1)}, f32[32,104]{1,0:T(8,128)S(1)}, bf16[3,8,2048]{2,1,0:T(8,128)(2,1)S(1)}) custom-call(bf16[3,8,2048]{2,1,0:T(8,128)(2,1)} %x_any.1, s32[3,8,64]{2,1,0:T(8,128)} %lab_any.1, bf16[4,32,864]{2,1,0:T(8,128)(2,1)} %bitcast.9, bf16[32,104]{1,0:T(8,128)(2,1)} %bitcast.10, s32[3,8]{1,0:T(4,128)} %match_any.1), custom_call_target="tpu_custom_call" | custom-call | tf_op jit(solution)/shard_map/pallas_call | solution.py:560
  60.7 0.8 %shard_map.77 = (f32[4,32,864]{2,1,0:T(8,128)}, f32[32,104]{1,0:T(8,128)}, bf16[3,8,2048]{2,1,0:T(8,128)(2,1)}) custom-call(f32[4,32,864]{2,1,0:T(8,128)S(1)} %get-tuple-element.9.cg_ref, f32[32,104]{1,0:T(8,128)S(1)} %get-tuple-element.10.hg_ref, bf16[3,8,2048]{2,1,0:T(8,128)(2,1)S(1)} %get-tuple-element.11.ig_ref), custom_call_target="tpu_custom_call" | custom-call | tf_op jit(solution)/shard_map/pallas_call | solution.py:577

commit v5 on v4

--- a/solution.py
+++ b/solution.py
@@ -32,7 +32,7 @@
     x_any, lab_any, w_any, head_any, match_any,
     cg_ref, hg_ref, ig_ref,
     x_ref, lab_ref, w_ref, head_ref, match_ref,
-    xh, gh, xo, go, wt, wpad, tmp, slo, slw, hcat, tcat, hd, hzin, hzout, hall, zin, zout, far_in, far_out, pick_in, pick_out, part,
+    xh, gh, xo, go, wt, wpad, tmp, slo, slw, hcat, tcat, hd, hzin, hzout, hall, zin, zout, far_in, far_out, pick_in, pick_out, acc, part,
     pk, rsin, dep, fin,
     in_s, halo_s, halo_r, hx_s, hx_r, ax_s, ax_r, z_s, z_r, bx_s, bx_r, bz_s, bz_r, rs_s, rs_r, dp_s, dp_r, ag_s, ag_r,
 ):
@@ -230,6 +230,50 @@
         )
         return spill(nn(cols, band), shape)
 
+    def ahead_of_depth(layer, buf, at, halo, back):
+        def planes(*ps):
+            return jnp.concatenate(
+                [
+                    jnp.concatenate([buf[at, p, j : j + rows + 2].reshape(-1, 128) for p in ps], axis=0)
+                    for j in range(3)
+                ],
+                axis=1,
+            )
+
+        def band(i):
+            if back:
+                at_ij = [3 * (2 - i) + 2 - j for j in range(3)]
+                return jnp.concatenate(
+                    [jnp.concatenate([weights(layer, ij, 0), weights(layer, ij, 1)], axis=1) for ij in at_ij], axis=0
+                )
+            return jnp.concatenate(
+                [
+                    jnp.concatenate([weights(layer, 3 * i + j, 0), weights(layer, 3 * i + j, 1)], axis=0)
+                    for j in range(3)
+                ],
+                axis=1,
+            )
+
+        dot = nn if back else nt
+        n = (rows + 2) * 16
+        arrive(halo[6:])
+        own = [dot(planes(*range(2, slab + 2)), band(i)) for i in range(3)]
+        for p in range(slab + 2):
+            terms = [own[i][(p + i - 2) * n : (p + i - 1) * n] for i in range(3) if 0 <= p + i - 2 < slab]
+            acc[p * n : (p + 1) * n] = functools.reduce(jnp.add, terms)
+        arrive(halo[:6])
+        first = dot(planes(0, 1), band(0))
+        middle = dot(planes(1, slab + 2), band(1))
+        final = dot(planes(slab + 2, slab + 3), band(2))
+        more = {0: first[:n] + middle[:n], 1: first[n:], slab: final[:n], slab + 1: middle[n:] + final[n:]}
+        return spill(
+            jnp.concatenate(
+                [acc[p * n : (p + 1) * n] + more[p] if p in more else acc[p * n : (p + 1) * n] for p in range(slab + 2)],
+                axis=0,
+            ),
+            wide,
+        )
+
     def silu(y):
         return (y / (1.0 + jnp.exp(-y))).astype(BF16)
 
@@ -244,8 +288,7 @@
     loads[4].wait()
 
     for pair in range(2):
-        arrive(halo)
-        y = forward(2 * pair, windows(xh, pair, wide, 0, OFFSETS), wide)
+        y = ahead_of_depth(2 * pair, xh, pair, halo, False)
         put_near(xo, pair, silu(y))
         y2 = forward(2 * pair + 1, windows(xo, pair, mine, 0, OFFSETS), mine)
         act = silu(y2)
@@ -451,8 +494,7 @@
     pk[3, 7 // own_chunks, 7 % own_chunks] = heads.astype(BF16)
     weight_grad(3, g, windows(xo, 1, mine, 0, OFFSETS))
     first = send_row([3])
-    arrive(halo)
-    g3 = backward(3, windows(gh, 1, wide, 0, mirrored), wide) * slw[1]
+    g3 = ahead_of_depth(3, gh, 1, halo, True) * slw[1]
     put_near(go, 1, g3)
     g2 = backward(2, windows(go, 1, mine, 0, mirrored), mine) * slo[0]
     gh[0, own_p, own_r] = g2.astype(BF16)
@@ -461,8 +503,7 @@
     weight_grad(1, g2, windows(xo, 0, mine, 0, OFFSETS))
     second = send_row([1, 2])
     first = send_depth([3], first)
-    arrive(halo)
-    g1 = backward(1, windows(gh, 0, wide, 0, mirrored), wide) * slw[0]
+    g1 = ahead_of_depth(1, gh, 0, halo, True) * slw[0]
     put_near(go, 0, g1)
     first = send_all([3], first)
     weight_grad(0, g1[1 : slab + 1, 1 : rows + 1], windows(xh, 0, mine, 1, OFFSETS))
@@ -473,9 +514,9 @@
     for d in range(slab):
         for b in range(16):
             ig_ref[d, :, b * 128 : (b + 1) * 128] = tmp[pl.ds(d * plane + b, rows, stride=16), :].astype(BF16)
+    last = send_depth([0], last)
     second = send_all([1, 2], second)
     finish([3], first)
-    last = send_depth([0], last)
     last = send_all([0], last)
     finish([1, 2], second)
     for copy in started:
@@ -540,6 +581,7 @@
             pltpu.VMEM((slab, rows * 8, 128), BF16),
             [pltpu.VMEM((nx, rows * 8, 128), BF16) for _ in range(slab)],
             pltpu.VMEM((nx, slab, rows * 8, 128), BF16),
+            pltpu.VMEM(((slab + 2) * (rows + 2) * 16, 256), F32),
             pltpu.VMEM((slab, rows * 16, 512), F32),
             pltpu.VMEM((layers, nr) + chunk, BF16),
             pltpu.VMEM((layers, nr) + chunk, BF16),

time: 61.6 us -> 58.6 us (0.951)
  Pallas kernels: 60.9 us -> 57.8 us
    pallas_call x1, Pallas kernels: 60 us -> 57 us  [body(): pl.pallas_call(functools.partial(kernel, sizes), out_shape=(pltpu.VMEM((l...]
where the time goes in v5:
time: 58.6 us; the launch traced here: 58.5 us
  Pallas kernels  57.8 us (99%)
  between operations  0.64 us (1%)
    pallas_call x1, Pallas kernels, body(): pl.pallas_call(functools.partial(kernel, sizes), out_shape=(pltpu.VMEM((l...  57 us

profile of v5, /device:TPU:1, one launch (start us, length us, event | category | flops | bytes accessed | tf_op | source)
XLA Modules:
  0.0 58.5 jit_solution(10008006700983201062)
XLA Ops:
  0.6 57.0 %shard_map.76 = (f32[4,32,864]{2,1,0:T(8,128)S(1)}, f32[32,104]{1,0:T(8,128)S(1)}, bf16[3,8,2048]{2,1,0:T(8,128)(2,1)S(1)}) custom-call(bf16[3,8,2048]{2,1,0:T(8,128)(2,1)} %x_any.1, s32[3,8,64]{2,1,0:T(8,128)} %lab_any.1, bf16[4,32,864]{2,1,0:T(8,128)(2,1)} %bitcast.9, bf16[32,104]{1,0:T(8,128)(2,1)} %bitcast.10, s32[3,8]{1,0:T(4,128)} %match_any.1), custom_call_target="tpu_custom_call" | custom-call | tf_op jit(solution)/shard_map/pallas_call | solution.py:602
  57.7 0.8 %shard_map.77 = (f32[4,32,864]{2,1,0:T(8,128)}, f32[32,104]{1,0:T(8,128)}, bf16[3,8,2048]{2,1,0:T(8,128)(2,1)}) custom-call(f32[4,32,864]{2,1,0:T(8,128)S(1)} %get-tuple-element.9.cg_ref, f32[32,104]{1,0:T(8,128)S(1)} %get-tuple-element.10.hg_ref, bf16[3,8,2048]{2,1,0:T(8,128)(2,1)S(1)} %get-tuple-element.11.ig_ref), custom_call_target="tpu_custom_call" | custom-call | tf_op jit(solution)/shard_map/pallas_call | solution.py:619

commit v6 on v5

--- a/solution.py
+++ b/solution.py
@@ -23,7 +23,7 @@
 
 
 def slope(pre):
-    s = 1.0 / (1.0 + jnp.exp(-pre))
+    s = 0.5 * jnp.tanh(0.5 * pre) + 0.5
     return s * (1.0 + pre * (1.0 - s))
 
 
@@ -91,15 +91,17 @@
             src_ref=src, dst_ref=dst, send_sem=send, recv_sem=recv, device_id=mate, device_id_type=MESH
         )
 
-    def start(copies):
-        for copy in copies:
-            copy.start()
-        started.extend(copies)
-        return copies
-
-    def arrive(copies):
-        for copy in copies:
-            copy.wait_recv()
+    def send(jobs, total, send_sem, recv_sem):
+        for src, dst, mate in jobs:
+            remote(src, dst, send_sem, recv_sem, mate).start()
+        if jobs:
+            whole = remote(total, total, send_sem, recv_sem, jobs[0][2])
+            started.append(whole)
+            return whole
+
+    def arrive(whole):
+        if whole is not None:
+            whole.wait_recv()
 
     loads[0].wait()
     for d in range(slab):
@@ -115,9 +117,9 @@
 
     pl.semaphore_wait(barrier, len(mates))
 
-    def halo_copies(buf, at, ex):
-        copies = []
-        for n, (dp, dr) in enumerate(NEIGHBOURS):
+    def send_halo(buf, at, ex):
+        jobs = []
+        for dp, dr in NEIGHBOURS:
             if dp == 0:
                 src_p, dst_p = pl.ds(2, slab), pl.ds(2, slab)
             elif dp == 1:
@@ -134,17 +136,15 @@
             else:
                 src_r = pl.ds(2, 2)
                 dst_r = pl.ds(jnp.where(row == 0, rows + 6, rows + 2), 2)
-            copies.append(
-                remote(
-                    buf.at[at, src_p, src_r], buf.at[at, dst_p, dst_r],
-                    halo_s.at[ex, n], halo_r.at[ex, n], near(dp, dr),
-                )
-            )
-        return copies
-
-    halo = start(halo_copies(xh, 0, 0))
-    head_x = start(
-        [remote(hd.at[xpos], hd.at[xpos], hx_s.at[s], hx_r.at[s], x_mate(s)) for s in range(1, nx)]
+            jobs.append((buf.at[at, src_p, src_r], buf.at[at, dst_p, dst_r], near(dp, dr)))
+        far = send(jobs[:6], buf.at[at, pl.ds(0, 4), pl.ds(0, rows + 4)], halo_s.at[ex, 0], halo_r.at[ex, 0])
+        beside = send(jobs[6:], buf.at[at, pl.ds(0, slab), pl.ds(0, 4)], halo_s.at[ex, 1], halo_r.at[ex, 1])
+        return far, beside
+
+    halo = send_halo(xh, 0, 0)
+    some_x = pl.ds(0, nx - 1)
+    head_x = send(
+        [(hd.at[xpos], hd.at[xpos], x_mate(s)) for s in range(1, nx)], hd.at[some_x], hx_s.at[0], hx_r.at[0]
     )
 
     def clear_wide(buf, at):
@@ -256,12 +256,12 @@
 
         dot = nn if back else nt
         n = (rows + 2) * 16
-        arrive(halo[6:])
+        arrive(halo[1])
         own = [dot(planes(*range(2, slab + 2)), band(i)) for i in range(3)]
         for p in range(slab + 2):
             terms = [own[i][(p + i - 2) * n : (p + i - 1) * n] for i in range(3) if 0 <= p + i - 2 < slab]
             acc[p * n : (p + 1) * n] = functools.reduce(jnp.add, terms)
-        arrive(halo[:6])
+        arrive(halo[0])
         first = dot(planes(0, 1), band(0))
         middle = dot(planes(1, slab + 2), band(1))
         final = dot(planes(slab + 2, slab + 3), band(2))
@@ -275,7 +275,7 @@
         )
 
     def silu(y):
-        return (y / (1.0 + jnp.exp(-y))).astype(BF16)
+        return (y * (0.5 * jnp.tanh(0.5 * y) + 0.5)).astype(BF16)
 
     def slope_of(y):
         return slope(y.astype(BF16).astype(F32))
@@ -294,26 +294,26 @@
         act = silu(y2)
         if pair == 0:
             xh[1, own_p, own_r] = act
-            halo = start(halo_copies(xh, 1, 1))
+            halo = send_halo(xh, 1, 1)
         else:
             for d in range(slab):
                 tiles = act[d].reshape(plane, 128)
                 hall[d][xpos] = tiles[:part_rows]
                 far_out[d] = tiles[part_rows:]
-            far = [start([remote(far_out.at[d], far_in.at[d], bz_s.at[d], bz_r.at[d], z_mate)]) for d in range(slab)]
+            far = [
+                send([(far_out.at[d], far_in.at[d], z_mate)], far_in.at[d], bz_s.at[d], bz_r.at[d]) for d in range(slab)
+            ]
             act_x = [
-                start(
-                    [
-                        remote(hall[d].at[xpos], hall[d].at[xpos], ax_s.at[d, s], ax_r.at[d, s], x_mate(s))
-                        for s in X_ORDER(nx)
-                    ]
+                send(
+                    [(hall[d].at[xpos], hall[d].at[xpos], x_mate(s)) for s in X_ORDER(nx)],
+                    hall[d].at[some_x], ax_s.at[d], ax_r.at[d],
                 )
                 for d in range(slab)
             ]
             arrive(head_x)
             for d in range(slab):
                 hzout[d] = hd[lax.div(match_ref[d, 2 * xpos + (1 - zhalf)], 2)]
-            head_z = start([remote(hzout, hzin, z_s.at[slab], z_r.at[slab], z_mate)])
+            head_z = send([(hzout, hzin, z_mate)], hzin, z_s.at[slab], z_r.at[slab])
         slw[pair] = slope_of(y)
         slo[pair] = slope_of(y2)
 
@@ -352,7 +352,7 @@
     for d in range(slab):
         arrive(act_x[d])
         zout[d] = hall[d][lax.div(match_ref[d, 2 * xpos + (1 - zhalf)], 2)]
-        act_z.append(start([remote(zout.at[d], zin.at[d], z_s.at[d], z_r.at[d], z_mate)]))
+        act_z.append(send([(zout.at[d], zin.at[d], z_mate)], zin.at[d], z_s.at[d], z_r.at[d]))
     act_b = []
     for d in range(slab):
         arrive(far[d])
@@ -366,43 +366,46 @@
             else:
                 pick_out[s, d] = chosen
         act_b.append(
-            start(
-                [
-                    remote(pick_out.at[s, d], pick_in[d].at[xpos], bx_s.at[d, s], bx_r.at[d, s], x_mate(s))
-                    for s in X_ORDER(nx)
-                ]
+            send(
+                [(pick_out.at[s, d], pick_in[d].at[xpos], x_mate(s)) for s in X_ORDER(nx)],
+                pick_in[d].at[some_x], bx_s.at[d], bx_r.at[d],
             )
         )
     arrive(head_z)
-    grad_rows = []
+    at_x, is_near = [], []
     for d in range(slab):
         source = match_ref[d, peer]
-        near_half = lax.rem(source, 2) == zhalf
-        near_at = lax.div(source, 2)
-        target_head = jnp.where(near_half, hd[near_at].astype(F32), hzin[d].astype(F32)).astype(BF16)
+        is_near.append(lax.rem(source, 2) == zhalf)
+        at_x.append(lax.div(source, 2))
+        target_head = jnp.where(is_near[d], hd[at_x[d]].astype(F32), hzin[d].astype(F32)).astype(BF16)
         for a in range(4):
             tcat[d, a * 32 : (a + 1) * 32, a * 128 : (a + 1) * 128] = target_head
+    g_planes, grad_rows = [], []
+    for d in range(slab):
         arrive(act_z[d])
         arrive(act_b[d])
         target_act = jnp.concatenate(
             [
-                jnp.where(near_half, hall[d][near_at].astype(F32), zin[d].astype(F32)).astype(BF16),
-                pick_in[d][near_at],
+                jnp.where(is_near[d], hall[d][at_x[d]].astype(F32), zin[d].astype(F32)).astype(BF16),
+                pick_in[d][at_x[d]],
             ],
             axis=0,
         )
         target = softmax(target_act, tcat[d])
-        grad_rows.append(
-            jnp.concatenate(
-                [
-                    (part[d, :, a * 128 : (a + 1) * 128] - 0.5 * target[a].astype(BF16).astype(F32)).astype(BF16)
-                    for a in range(4)
-                ],
-                axis=1,
-            )
-        )
+        grad = jnp.concatenate(
+            [
+                (part[d, :, a * 128 : (a + 1) * 128] - 0.5 * target[a].astype(BF16).astype(F32)).astype(BF16)
+                for a in range(4)
+            ],
+            axis=1,
+        )
+        grad_rows.append(grad)
+        g_d = nt(grad, hcat[...]).reshape(rows, 16, 128) * slo[1, d]
+        gh[1, 2 + d, own_r] = g_d.astype(BF16)
+        g_planes.append(g_d)
+    halo = send_halo(gh, 1, 3)
     dlogits = jnp.concatenate(grad_rows, axis=0)
-    g = nt(dlogits, hcat[...]).reshape(slab, rows, 16, 128) * slo[1]
+    g = jnp.stack(g_planes)
 
     group32 = lax.div(lax.broadcasted_iota(jnp.int32, (32, 128), 1), 32)
     group288 = lax.div(lax.broadcasted_iota(jnp.int32, (288, 128), 1), 32)
@@ -415,13 +418,13 @@
         ahead = jnp.where(from_next & (block < 15), pltpu.roll(g, 15, 1), 0.0)
         edge = jnp.where(from_last & (block > 0), pltpu.roll(g, 1, 1), ahead)
         both = jnp.concatenate([g.reshape(cells, 128), edge.reshape(cells, 128)], axis=1).astype(BF16).T
-        prod = nn(both, cols)
+        prod = nn(jnp.concatenate([both[0:160], both[224:256]], axis=0), cols)
 
         def take(at):
             return jnp.concatenate([prod[at : at + 32, ij * 128 : (ij + 1) * 128] for ij in range(9)], axis=0)
 
         s0 = jnp.where(group288 == 3, take(128), take(0))
-        s3 = jnp.where(group288 == 0, take(224), take(96))
+        s3 = jnp.where(group288 == 0, take(160), take(96))
         total = take(32) + pltpu.roll(s0, 32, 1) + pltpu.roll(take(64), 96, 1) + pltpu.roll(s3, 64, 1)
         for t in range(7):
             tile = None
@@ -435,49 +438,43 @@
             pk[layer, 7 // own_chunks, 7 % own_chunks] = jnp.zeros((32, 128), BF16)
 
     def span(layer_set):
-        return pl.ds(layer_set[0], len(layer_set)), layer_set[0]
+        return pl.ds(layer_set[0], len(layer_set)), min(layer_set[0], layers - 2)
 
     def send_row(layer_set):
         at, n = span(layer_set)
-        return start(
-            [
-                remote(pk.at[at, lax.rem(row + s, nr)], rsin.at[at, s], rs_s.at[n, s], rs_r.at[n, s], row_mate(s))
-                for s in range(1, nr)
-            ]
-        )
-
-    def send_depth(layer_set, copies):
-        arrive(copies)
+        return send(
+            [(pk.at[at, lax.rem(row + s, nr)], rsin.at[at, s], row_mate(s)) for s in range(1, nr)],
+            rsin.at[at, pl.ds(1, nr - 1)], rs_s.at[n], rs_r.at[n],
+        )
+
+    def send_depth(layer_set, whole):
+        arrive(whole)
         at, n = span(layer_set)
         for layer in layer_set:
             total = pk[layer, row].astype(F32)
             for s in range(1, nr):
                 total = total + rsin[layer, s].astype(F32)
             dep[layer, depth] = total.astype(BF16)
-        return start(
-            [
-                remote(dep.at[at, depth], dep.at[at, depth], dp_s.at[n, s], dp_r.at[n, s], depth_mate(s))
-                for s in range(1, nd)
-            ]
-        )
-
-    def send_all(layer_set, copies):
-        arrive(copies)
+        return send(
+            [(dep.at[at, depth], dep.at[at, depth], depth_mate(s)) for s in range(1, nd)],
+            dep.at[at, pl.ds(0, nd - 1)], dp_s.at[n], dp_r.at[n],
+        )
+
+    def send_all(layer_set, whole):
+        arrive(whole)
         at, n = span(layer_set)
         for layer in layer_set:
             total = dep[layer, 0].astype(F32)
             for s in range(1, nd):
                 total = total + dep[layer, s].astype(F32)
             fin[layer, row] = total.astype(BF16)
-        return start(
-            [
-                remote(fin.at[at, row], fin.at[at, row], ag_s.at[n, s], ag_r.at[n, s], row_mate(s))
-                for s in range(1, nr)
-            ]
-        )
-
-    def finish(layer_set, copies):
-        arrive(copies)
+        return send(
+            [(fin.at[at, row], fin.at[at, row], row_mate(s)) for s in range(1, nr)],
+            fin.at[at, pl.ds(0, nr - 1)], ag_s.at[n], ag_r.at[n],
+        )
+
+    def finish(layer_set, whole):
+        arrive(whole)
         for layer in layer_set:
             for t in range(7):
                 lanes = min(128, 27 * 32 - t * 128)
@@ -485,8 +482,6 @@
             if layer == layers - 1:
                 hg_ref[...] = fin[layer, 7 // own_chunks, 7 % own_chunks].astype(F32)[:, :classes]
 
-    gh[1, own_p, own_r] = g.astype(BF16)
-    halo = start(halo_copies(gh, 1, 3))
     wide_heads = nn(hidden.T, dlogits)
     heads = wide_heads[0:32, 0:128]
     for a in range(1, 4):
@@ -498,7 +493,7 @@
     put_near(go, 1, g3)
     g2 = backward(2, windows(go, 1, mine, 0, mirrored), mine) * slo[0]
     gh[0, own_p, own_r] = g2.astype(BF16)
-    halo = start(halo_copies(gh, 0, 2))
+    halo = send_halo(gh, 0, 2)
     weight_grad(2, g3[1 : slab + 1, 1 : rows + 1], windows(xh, 1, mine, 1, OFFSETS))
     weight_grad(1, g2, windows(xo, 0, mine, 0, OFFSETS))
     second = send_row([1, 2])
@@ -519,15 +514,17 @@
     finish([3], first)
     last = send_all([0], last)
     finish([1, 2], second)
-    for copy in started:
-        copy.wait_send()
+    for whole in started:
+        whole.wait_send()
     finish([0], last)
 
 
 def write_out(cg_ref, hg_ref, ig_ref, cg_out, hg_out, ig_out, sem):
     copies = [
         pltpu.make_async_copy(src, dst, sem.at[n])
-        for n, (src, dst) in enumerate([(cg_ref, cg_out), (ig_ref, ig_out), (hg_ref, hg_out)])
+        for n, (src, dst) in enumerate(
+            [(cg_ref.at[i], cg_out.at[i]) for i in range(cg_ref.shape[0])] + [(ig_ref, ig_out), (hg_ref, hg_out)]
+        )
     ]
     for copy in copies:
         copy.start()
@@ -588,15 +585,15 @@
             pltpu.VMEM((layers, nd) + chunk, BF16),
             pltpu.VMEM((layers, nr) + chunk, BF16),
             dma((5,)),
-            dma((4, 8)), dma((4, 8)),
-            dma((nx,)), dma((nx,)),
-            dma((slab, nx)), dma((slab, nx)),
+            dma((4, 2)), dma((4, 2)),
+            dma((1,)), dma((1,)),
+            dma((slab,)), dma((slab,)),
             dma((slab + 1,)), dma((slab + 1,)),
-            dma((slab, nx)), dma((slab, nx)),
             dma((slab,)), dma((slab,)),
-            dma((layers, nr)), dma((layers, nr)),
-            dma((layers, nd)), dma((layers, nd)),
-            dma((layers, nr)), dma((layers, nr)),
+            dma((slab,)), dma((slab,)),
+            dma((layers - 1,)), dma((layers - 1,)),
+            dma((layers - 1,)), dma((layers - 1,)),
+            dma((layers - 1,)), dma((layers - 1,)),
         ]
         sizes = (nx, nd, nr, slab, rows, classes, layers)
         cg, hg, ig = pl.pallas_call(
@@ -621,7 +618,7 @@
             out_shape=tuple(jax.ShapeDtypeStruct(v.shape, v.dtype) for v in (cg, hg, ig)),
             in_specs=[vmem] * 3,
             out_specs=(hbm,) * 3,
-            scratch_shapes=[dma((3,))],
+            scratch_shapes=[dma((layers + 2,))],
             compiler_params=pltpu.CompilerParams(vmem_limit_bytes=2**20),
         )(cg, hg, ig)
         return cg.transpose(0, 2, 1)[None], hg[None], ig[None]

time: 58.6 us -> 56.3 us (0.961)
  Pallas kernels: 57.8 us -> 55.5 us
    pallas_call x1, Pallas kernels: 57 us -> 54.7 us  [body(): pl.pallas_call(functools.partial(kernel, sizes), out_shape=(pltpu.VMEM((l...]
where the time goes in v6:
time: 56.3 us; the launch traced here: 56.2 us
  Pallas kernels  55.5 us (99%)
  between operations  0.64 us (1%)
    pallas_call x1, Pallas kernels, body(): pl.pallas_call(functools.partial(kernel, sizes), out_shape=(pltpu.VMEM((l...  54.7 us

profile of v6, /device:TPU:1, one launch (start us, length us, event | category | flops | bytes accessed | tf_op | source)
XLA Modules:
  0.0 56.2 jit_solution(16005888110579009206)
XLA Ops:
  0.6 54.7 %shard_map.76 = (f32[4,32,864]{2,1,0:T(8,128)S(1)}, f32[32,104]{1,0:T(8,128)S(1)}, bf16[3,8,2048]{2,1,0:T(8,128)(2,1)S(1)}) custom-call(bf16[3,8,2048]{2,1,0:T(8,128)(2,1)} %x_any.1, s32[3,8,64]{2,1,0:T(8,128)} %lab_any.1, bf16[4,32,864]{2,1,0:T(8,128)(2,1)} %bitcast.9, bf16[32,104]{1,0:T(8,128)(2,1)} %bitcast.10, s32[3,8]{1,0:T(4,128)} %match_any.1), custom_call_target="tpu_custom_call" | custom-call | tf_op jit(solution)/shard_map/pallas_call | solution.py:599
  55.3 0.8 %shard_map.77 = (f32[4,32,864]{2,1,0:T(8,128)}, f32[32,104]{1,0:T(8,128)}, bf16[3,8,2048]{2,1,0:T(8,128)(2,1)}) custom-call(f32[4,32,864]{2,1,0:T(8,128)S(1)} %get-tuple-element.9.cg_ref, f32[32,104]{1,0:T(8,128)S(1)} %get-tuple-element.10.hg_ref, bf16[3,8,2048]{2,1,0:T(8,128)(2,1)S(1)} %get-tuple-element.11.ig_ref), custom_call_target="tpu_custom_call" | custom-call | tf_op jit(solution)/shard_map/pallas_call | solution.py:616

commit v7 on v6

--- a/solution.py
+++ b/solution.py
@@ -118,16 +118,15 @@
     pl.semaphore_wait(barrier, len(mates))
 
     def send_halo(buf, at, ex):
-        jobs = []
-        for dp, dr in NEIGHBOURS:
+        def job(dp, dr, step):
             if dp == 0:
                 src_p, dst_p = pl.ds(2, slab), pl.ds(2, slab)
             elif dp == 1:
-                src_p = pl.ds(slab, 2)
-                dst_p = pl.ds(jnp.where(depth == nd - 1, slab + 4, 0), 2)
+                src_p = pl.ds(slab + 1 - step, 1)
+                dst_p = pl.ds(jnp.where(depth == nd - 1, slab + 4, 0) + 1 - step, 1)
             else:
-                src_p = pl.ds(2, 2)
-                dst_p = pl.ds(jnp.where(depth == 0, slab + 6, slab + 2), 2)
+                src_p = pl.ds(2 + step, 1)
+                dst_p = pl.ds(jnp.where(depth == 0, slab + 6, slab + 2) + step, 1)
             if dr == 0:
                 src_r, dst_r = pl.ds(2, rows), pl.ds(2, rows)
             elif dr == 1:
@@ -136,10 +135,19 @@
             else:
                 src_r = pl.ds(2, 2)
                 dst_r = pl.ds(jnp.where(row == 0, rows + 6, rows + 2), 2)
-            jobs.append((buf.at[at, src_p, src_r], buf.at[at, dst_p, dst_r], near(dp, dr)))
-        far = send(jobs[:6], buf.at[at, pl.ds(0, 4), pl.ds(0, rows + 4)], halo_s.at[ex, 0], halo_r.at[ex, 0])
-        beside = send(jobs[6:], buf.at[at, pl.ds(0, slab), pl.ds(0, 4)], halo_s.at[ex, 1], halo_r.at[ex, 1])
-        return far, beside
+            return buf.at[at, src_p, src_r], buf.at[at, dst_p, dst_r], near(dp, dr)
+
+        beside = send(
+            [job(*step, 0) for step in NEIGHBOURS[6:]], buf.at[at, pl.ds(0, slab), pl.ds(0, 4)], halo_s.at[ex, 2], halo_r.at[ex, 2]
+        )
+        planes = [
+            send(
+                [job(*step, n) for step in NEIGHBOURS[:6]],
+                buf.at[at, pl.ds(0, 2), pl.ds(0, rows + 4)], halo_s.at[ex, n], halo_r.at[ex, n],
+            )
+            for n in range(2)
+        ]
+        return beside, *planes
 
     halo = send_halo(xh, 0, 0)
     some_x = pl.ds(0, nx - 1)
@@ -155,8 +163,7 @@
         buf[at, 0 : slab + 4, pl.ds(jnp.where(row == 0, 0, rows + 4), 2)] = zero_r
         buf[at, 0 : slab + 4, pl.ds(jnp.where(row == nr - 1, rows + 2, rows + 6), 2)] = zero_r
 
-    def put_near(buf, at, value):
-        buf[at, 0 : slab + 2, 0 : rows + 2] = value.astype(BF16)
+    def clear_near(buf, at):
         zero_p = jnp.zeros((1, rows + 2, 16, 128), BF16)
         buf[at, pl.ds(jnp.where(depth == 0, 0, slab + 2), 1), 0 : rows + 2] = zero_p
         buf[at, pl.ds(jnp.where(depth == nd - 1, slab + 1, slab + 3), 1), 0 : rows + 2] = zero_p
@@ -230,7 +237,7 @@
         )
         return spill(nn(cols, band), shape)
 
-    def ahead_of_depth(layer, buf, at, halo, back):
+    def ahead_of_depth(layer, buf, at, halo, back, emit):
         def planes(*ps):
             return jnp.concatenate(
                 [
@@ -256,23 +263,25 @@
 
         dot = nn if back else nt
         n = (rows + 2) * 16
-        arrive(halo[1])
+        arrive(halo[0])
         own = [dot(planes(*range(2, slab + 2)), band(i)) for i in range(3)]
         for p in range(slab + 2):
             terms = [own[i][(p + i - 2) * n : (p + i - 1) * n] for i in range(3) if 0 <= p + i - 2 < slab]
             acc[p * n : (p + 1) * n] = functools.reduce(jnp.add, terms)
-        arrive(halo[0])
-        first = dot(planes(0, 1), band(0))
+        arrive(halo[1])
+        inner = [
+            acc[n : 2 * n] + dot(planes(1), band(0)),
+            acc[2 * n : slab * n],
+            acc[slab * n : (slab + 1) * n] + dot(planes(slab + 2), band(2)),
+        ]
+        emit(spill(jnp.concatenate(inner, axis=0), (slab, rows + 2)), 1)
         middle = dot(planes(1, slab + 2), band(1))
-        final = dot(planes(slab + 2, slab + 3), band(2))
-        more = {0: first[:n] + middle[:n], 1: first[n:], slab: final[:n], slab + 1: middle[n:] + final[n:]}
-        return spill(
-            jnp.concatenate(
-                [acc[p * n : (p + 1) * n] + more[p] if p in more else acc[p * n : (p + 1) * n] for p in range(slab + 2)],
-                axis=0,
-            ),
-            wide,
-        )
+        acc[0:n] = acc[0:n] + middle[:n]
+        acc[(slab + 1) * n : (slab + 2) * n] = acc[(slab + 1) * n : (slab + 2) * n] + middle[n:]
+        yield
+        arrive(halo[2])
+        emit(spill(acc[0:n] + dot(planes(0), band(0)), (1, rows + 2)), 0)
+        emit(spill(acc[(slab + 1) * n : (slab + 2) * n] + dot(planes(slab + 3), band(2)), (1, rows + 2)), slab + 1)
 
     def silu(y):
         return (y * (0.5 * jnp.tanh(0.5 * y) + 0.5)).astype(BF16)
@@ -281,15 +290,21 @@
         return slope(y.astype(BF16).astype(F32))
 
     mine = (slab, rows)
-    wide = (slab + 2, rows + 2)
     mirrored = [(2 - i, 2 - j) for i, j in OFFSETS]
 
     loads[3].wait()
     loads[4].wait()
 
     for pair in range(2):
-        y = ahead_of_depth(2 * pair, xh, pair, halo, False)
-        put_near(xo, pair, silu(y))
+        wide_y = {}
+
+        def emit_act(y, p, pair=pair, wide_y=wide_y):
+            xo[pair, p : p + y.shape[0], 0 : rows + 2] = silu(y)
+            wide_y[p] = y
+
+        for _ in ahead_of_depth(2 * pair, xh, pair, halo, False, emit_act):
+            pass
+        clear_near(xo, pair)
         y2 = forward(2 * pair + 1, windows(xo, pair, mine, 0, OFFSETS), mine)
         act = silu(y2)
         if pair == 0:
@@ -314,7 +329,8 @@
             for d in range(slab):
                 hzout[d] = hd[lax.div(match_ref[d, 2 * xpos + (1 - zhalf)], 2)]
             head_z = send([(hzout, hzin, z_mate)], hzin, z_s.at[slab], z_r.at[slab])
-        slw[pair] = slope_of(y)
+        for p, y in wide_y.items():
+            slw[pair, p : p + y.shape[0]] = slope_of(y)
         slo[pair] = slope_of(y2)
 
     hidden = act.reshape(cells, 128)
@@ -382,8 +398,9 @@
             tcat[d, a * 32 : (a + 1) * 32, a * 128 : (a + 1) * 128] = target_head
     g_planes, grad_rows = [], []
     for d in range(slab):
-        arrive(act_z[d])
-        arrive(act_b[d])
+        for due in {0: [0], 1: range(1, slab)}.get(d, []):
+            arrive(act_z[due])
+            arrive(act_b[due])
         target_act = jnp.concatenate(
             [
                 jnp.where(is_near[d], hall[d][at_x[d]].astype(F32), zin[d].astype(F32)).astype(BF16),
@@ -440,10 +457,12 @@
     def span(layer_set):
         return pl.ds(layer_set[0], len(layer_set)), min(layer_set[0], layers - 2)
 
+    far_first = sorted(range(1, nr), key=lambda s: -min(s, nr - s))
+
     def send_row(layer_set):
         at, n = span(layer_set)
         return send(
-            [(pk.at[at, lax.rem(row + s, nr)], rsin.at[at, s], row_mate(s)) for s in range(1, nr)],
+            [(pk.at[at, lax.rem(row + s, nr)], rsin.at[at, s], row_mate(s)) for s in far_first],
             rsin.at[at, pl.ds(1, nr - 1)], rs_s.at[n], rs_r.at[n],
         )
 
@@ -469,7 +488,7 @@
                 total = total + dep[layer, s].astype(F32)
             fin[layer, row] = total.astype(BF16)
         return send(
-            [(fin.at[at, row], fin.at[at, row], row_mate(s)) for s in range(1, nr)],
+            [(fin.at[at, row], fin.at[at, row], row_mate(s)) for s in far_first],
             fin.at[at, pl.ds(0, nr - 1)], ag_s.at[n], ag_r.at[n],
         )
 
@@ -489,20 +508,32 @@
     pk[3, 7 // own_chunks, 7 % own_chunks] = heads.astype(BF16)
     weight_grad(3, g, windows(xo, 1, mine, 0, OFFSETS))
     first = send_row([3])
-    g3 = ahead_of_depth(3, gh, 1, halo, True) * slw[1]
-    put_near(go, 1, g3)
+    inner_g = {}
+
+    def emit_grad(at):
+        def emit(y, p):
+            g = y * slw[at, p : p + y.shape[0]]
+            go[at, p : p + y.shape[0], 0 : rows + 2] = g.astype(BF16)
+            if p == 1:
+                inner_g[at] = g[:, 1 : rows + 1]
+
+        return emit
+
+    for _ in ahead_of_depth(3, gh, 1, halo, True, emit_grad(1)):
+        pass
+    clear_near(go, 1)
     g2 = backward(2, windows(go, 1, mine, 0, mirrored), mine) * slo[0]
     gh[0, own_p, own_r] = g2.astype(BF16)
     halo = send_halo(gh, 0, 2)
-    weight_grad(2, g3[1 : slab + 1, 1 : rows + 1], windows(xh, 1, mine, 1, OFFSETS))
+    weight_grad(2, inner_g[1], windows(xh, 1, mine, 1, OFFSETS))
     weight_grad(1, g2, windows(xo, 0, mine, 0, OFFSETS))
     second = send_row([1, 2])
     first = send_depth([3], first)
-    g1 = ahead_of_depth(1, gh, 0, halo, True) * slw[0]
-    put_near(go, 0, g1)
+    for _ in ahead_of_depth(1, gh, 0, halo, True, emit_grad(0)):
+        weight_grad(0, inner_g[0], windows(xh, 0, mine, 1, OFFSETS))
+        last = send_row([0])
+    clear_near(go, 0)
     first = send_all([3], first)
-    weight_grad(0, g1[1 : slab + 1, 1 : rows + 1], windows(xh, 0, mine, 1, OFFSETS))
-    last = send_row([0])
     second = send_depth([1, 2], second)
     back = backward(0, windows(go, 0, mine, 0, mirrored), mine)
     tmp[...] = back.reshape(cells, 128)
@@ -522,9 +553,7 @@
 def write_out(cg_ref, hg_ref, ig_ref, cg_out, hg_out, ig_out, sem):
     copies = [
         pltpu.make_async_copy(src, dst, sem.at[n])
-        for n, (src, dst) in enumerate(
-            [(cg_ref.at[i], cg_out.at[i]) for i in range(cg_ref.shape[0])] + [(ig_ref, ig_out), (hg_ref, hg_out)]
-        )
+        for n, (src, dst) in enumerate([(cg_ref, cg_out), (ig_ref, ig_out), (hg_ref, hg_out)])
     ]
     for copy in copies:
         copy.start()
@@ -585,7 +614,7 @@
             pltpu.VMEM((layers, nd) + chunk, BF16),
             pltpu.VMEM((layers, nr) + chunk, BF16),
             dma((5,)),
-            dma((4, 2)), dma((4, 2)),
+            dma((4, 3)), dma((4, 3)),
             dma((1,)), dma((1,)),
             dma((slab,)), dma((slab,)),
             dma((slab + 1,)), dma((slab + 1,)),
@@ -618,7 +647,7 @@
             out_shape=tuple(jax.ShapeDtypeStruct(v.shape, v.dtype) for v in (cg, hg, ig)),
             in_specs=[vmem] * 3,
             out_specs=(hbm,) * 3,
-            scratch_shapes=[dma((layers + 2,))],
+            scratch_shapes=[dma((3,))],
             compiler_params=pltpu.CompilerParams(vmem_limit_bytes=2**20),
         )(cg, hg, ig)
         return cg.transpose(0, 2, 1)[None], hg[None], ig[None]

time: 56.3 us -> 54.8 us (0.973)
  Pallas kernels: 55.5 us -> 54.1 us
    pallas_call x1, Pallas kernels: 54.7 us -> 53.3 us  [body(): pl.pallas_call(functools.partial(kernel, sizes), out_shape=(pltpu.VMEM((l...]
where the time goes in v7:
time: 54.8 us; the launch traced here: 54.7 us
  Pallas kernels  54.1 us (99%)
  between operations  0.64 us (1%)
    pallas_call x1, Pallas kernels, body(): pl.pallas_call(functools.partial(kernel, sizes), out_shape=(pltpu.VMEM((l...  53.3 us

profile of v7, /device:TPU:1, one launch (start us, length us, event | category | flops | bytes accessed | tf_op | source)
XLA Modules:
  0.0 54.7 jit_solution(10111781297222113298)
XLA Ops:
  0.6 53.3 %shard_map.76 = (f32[4,32,864]{2,1,0:T(8,128)S(1)}, f32[32,104]{1,0:T(8,128)S(1)}, bf16[3,8,2048]{2,1,0:T(8,128)(2,1)S(1)}) custom-call(bf16[3,8,2048]{2,1,0:T(8,128)(2,1)} %x_any.1, s32[3,8,64]{2,1,0:T(8,128)} %lab_any.1, bf16[4,32,864]{2,1,0:T(8,128)(2,1)} %bitcast.9, bf16[32,104]{1,0:T(8,128)(2,1)} %bitcast.10, s32[3,8]{1,0:T(4,128)} %match_any.1), custom_call_target="tpu_custom_call" | custom-call | tf_op jit(solution)/shard_map/pallas_call | solution.py:628
  53.9 0.8 %shard_map.77 = (f32[4,32,864]{2,1,0:T(8,128)}, f32[32,104]{1,0:T(8,128)}, bf16[3,8,2048]{2,1,0:T(8,128)(2,1)}) custom-call(f32[4,32,864]{2,1,0:T(8,128)S(1)} %get-tuple-element.9.cg_ref, f32[32,104]{1,0:T(8,128)S(1)} %get-tuple-element.10.hg_ref, bf16[3,8,2048]{2,1,0:T(8,128)(2,1)S(1)} %get-tuple-element.11.ig_ref), custom_call_target="tpu_custom_call" | custom-call | tf_op jit(solution)/shard_map/pallas_call | solution.py:645

commit v8 on v7

--- a/solution.py
+++ b/solution.py
@@ -533,7 +533,6 @@
         weight_grad(0, inner_g[0], windows(xh, 0, mine, 1, OFFSETS))
         last = send_row([0])
     clear_near(go, 0)
-    first = send_all([3], first)
     second = send_depth([1, 2], second)
     back = backward(0, windows(go, 0, mine, 0, mirrored), mine)
     tmp[...] = back.reshape(cells, 128)
@@ -541,9 +540,10 @@
         for b in range(16):
             ig_ref[d, :, b * 128 : (b + 1) * 128] = tmp[pl.ds(d * plane + b, rows, stride=16), :].astype(BF16)
     last = send_depth([0], last)
+    first = send_all([3], first)
     second = send_all([1, 2], second)
+    last = send_all([0], last)
     finish([3], first)
-    last = send_all([0], last)
     finish([1, 2], second)
     for whole in started:
         whole.wait_send()

time: 54.8 us -> 54.7 us (level)
  no operation moved by 1% of the time
where the time goes in v8:
time: 54.7 us; the launch traced here: 54.6 us
  Pallas kernels  54 us (99%)
  between operations  0.64 us (1%)
    pallas_call x1, Pallas kernels, body(): pl.pallas_call(functools.partial(kernel, sizes), out_shape=(pltpu.VMEM((l...  53.2 us

profile of v8, /device:TPU:1, one launch (start us, length us, event | category | flops | bytes accessed | tf_op | source)
XLA Modules:
  0.0 54.6 jit_solution(3473528182272892438)
XLA Ops:
  0.6 53.2 %shard_map.76 = (f32[4,32,864]{2,1,0:T(8,128)S(1)}, f32[32,104]{1,0:T(8,128)S(1)}, bf16[3,8,2048]{2,1,0:T(8,128)(2,1)S(1)}) custom-call(bf16[3,8,2048]{2,1,0:T(8,128)(2,1)} %x_any.1, s32[3,8,64]{2,1,0:T(8,128)} %lab_any.1, bf16[4,32,864]{2,1,0:T(8,128)(2,1)} %bitcast.9, bf16[32,104]{1,0:T(8,128)(2,1)} %bitcast.10, s32[3,8]{1,0:T(4,128)} %match_any.1), custom_call_target="tpu_custom_call" | custom-call | tf_op jit(solution)/shard_map/pallas_call | solution.py:628
  53.8 0.8 %shard_map.77 = (f32[4,32,864]{2,1,0:T(8,128)}, f32[32,104]{1,0:T(8,128)}, bf16[3,8,2048]{2,1,0:T(8,128)(2,1)}) custom-call(f32[4,32,864]{2,1,0:T(8,128)S(1)} %get-tuple-element.9.cg_ref, f32[32,104]{1,0:T(8,128)S(1)} %get-tuple-element.10.hg_ref, bf16[3,8,2048]{2,1,0:T(8,128)(2,1)S(1)} %get-tuple-element.11.ig_ref), custom_call_target="tpu_custom_call" | custom-call | tf_op jit(solution)/shard_map/pallas_call | solution.py:645
